TPU v7x, 512 devices: a whole 4x8x8 slice. The times are simulated.
512 devices in a mesh: dp: 64 (over x, z, y_lo), tp: 8 (over y_hi, core).
Axes of the slice: x: 4, y: 8 (y_hi: 4, y_lo: 2; y = y_hi * 2 + y_lo), z: 8, core: 2. Of those that a mesh axis runs over, the one named last changes fastest.
Arguments:
- stash_values: bfloat16 [65536, 8192], P(('dp', 'tp')), may hold values from -127 to 127
- stash_scales: bfloat16 [65536, 64], P(('dp', 'tp')), may hold values from 0.001 to 0.13
- value_grad: bfloat16 [65536, 1024], P('dp', 'tp'), may hold values from -19 to 19
Outputs:
- clipped_grad: float32 [8192, 1024], P('dp', 'tp')
All inputs are finite; a program needn't handle non-finite values.
Results may differ from a plain program's by a relative error of at most 0.0019.
Values may be sent and summed in bfloat16 or wider, within the bound.
A program may use at most 64 MiB of HBM per device.

v0:
```python
import jax
import jax.numpy as jnp
from jax import lax
from jax.sharding import Mesh
from jax.sharding import PartitionSpec as P

DP = ("dp_0", "dp_1", "dp_2")
TP = ("tp_0", "tp_1")
DP_TP = ("dp_0", "dp_1", "dp_2", "tp_0", "tp_1")


def copy_for_each(shard, axis):
    copies = jnp.broadcast_to(shard, (lax.axis_size(axis), *shard.shape))
    return lax.all_to_all(copies, axis, split_axis=0, concat_axis=0, tiled=True)


def in_order(pieces, dim):
    pieces = jnp.moveaxis(pieces, 0, dim)
    shape = pieces.shape
    return pieces.reshape(*shape[:dim], shape[dim] * shape[dim + 1], *shape[dim + 2 :])


def collect(shard, axis, dim):
    pieces = copy_for_each(shard, axis)
    return in_order(pieces, dim)


def split_up(shard, dim, size):
    shape = shard.shape
    pieces = shard.reshape(*shape[:dim], size, shape[dim] // size, *shape[dim + 1 :])
    return jnp.moveaxis(pieces, dim, 0)


def sent_and_summed(shard, axis, dim):
    pieces = split_up(shard, dim, lax.axis_size(axis))
    arrived = lax.all_to_all(pieces, axis, split_axis=0, concat_axis=0, tiled=True)
    return arrived.astype(jnp.float32).sum(axis=0)


def over_axes(shard, axes):
    for axis in axes:
        shard = lax.psum(shard, axis)
    return shard


def block_dequantize(values, scales):
    rows = values.shape[0]
    blocks = scales.shape[1]
    scaled = (
        values.astype(jnp.float32).reshape(rows, blocks, values.shape[1] // blocks)
        * scales.astype(jnp.float32)[:, :, None]
    )
    return scaled.reshape(rows, values.shape[1]).astype(jnp.bfloat16)


def body(stash_values, stash_scales, value_grad):
    width = stash_values.shape[1]
    columns = value_grad.shape[1]
    dp_count = lax.axis_size(DP)
    tp_count = lax.axis_size(TP)
    own_tokens = stash_values.shape[0]
    sub_rows = width // (dp_count * tp_count)
    inputs = block_dequantize(stash_values, stash_scales)
    inputs = inputs.reshape(own_tokens, dp_count, tp_count, sub_rows)
    features = lax.all_to_all(inputs, TP, split_axis=2, concat_axis=0, tiled=True)
    features = features.reshape(own_tokens * tp_count, dp_count * sub_rows)
    all_heads = lax.dot_general(
        features,
        collect(value_grad, TP, 1),
        (((0,), (0,)), ((), ())),
        preferred_element_type=jnp.float32,
    )
    summed = sent_and_summed(all_heads.astype(jnp.bfloat16), DP, 0)
    local = lax.all_to_all(summed, TP, split_axis=1, concat_axis=0, tiled=True)
    total = over_axes(jnp.sum(summed * summed), DP_TP)
    limit = jnp.sqrt(jnp.float32(width * columns * lax.axis_size(TP)))
    return local * jnp.minimum(jnp.float32(1.0), limit / jnp.sqrt(total))


def solution(mesh):
    torus = Mesh(mesh.devices.reshape(4, 8, 2, 4, 2), ("dp_0", "dp_1", "dp_2", "tp_0", "tp_1"))
    return jax.shard_map(
        body,
        mesh=torus,
        in_specs=(P(DP_TP, None), P(DP_TP, None), P(DP, TP)),
        out_specs=P(DP, TP),
        check_vma=False,
    )
```

profile of v0, /device:TPU:1, one launch (start us, length us, event | category | flops | bytes accessed | tf_op | source)
XLA Modules:
  0.0 247.4 jit_solution(15634709426231722610)
XLA Ops:
  0.0 0.7 convert_element_type.16
  0.7 3.2 %copy.12 = bf16[128,8192]{0,1:T(8,128)(2,1)S(1)} copy(bf16[128,8192]{1,0:T(8,128)(2,1)} %param.3) | data formatting | bytes 4194304 | tf_op args[0]
  3.9 0.4 fusion
  4.4 1.7 copy.13
  6.1 0.0 copy-start
  6.1 10.5 %all-to-all-start = ((bf16[128,64,8,16]{0,3,1,2:T(8,128)(2,1)}), bf16[128,64,8,16]{0,3,1,2:T(8,128)(2,1)S(1)}, u32[]{:S(2)}, u32[]{:S(2)}) async-start(bf16[128,64,8,16]{0,3,1,2:T(8,128)(2,1)} %copy.13), calls=%async_computation | async-start | bytes 4194304 | tf_op jit(solution)/shard_map/all_to_all | solution.py:65
  16.6 0.0 copy-done
  16.6 0.1 copy.15
  16.7 48.7 %all-to-all-done = bf16[128,64,8,16]{0,3,1,2:T(8,128)(2,1)S(1)} async-done(((bf16[128,64,8,16]{0,3,1,2:T(8,128)(2,1)}), bf16[128,64,8,16]{0,3,1,2:T(8,128)(2,1)S(1)}, u32[]{:S(2)}, u32[]{:S(2)}) %all-to-all-start) | async-done | bytes 2097184 | tf_op jit(solution)/shard_map/all_to_all | solution.py:65
  65.4 1.6 broadcast_in_dim.4
  67.0 5.0 %all-to-all-start.1 = ((bf16[8,1024,128]{1,2,0:T(8,128)(2,1)}), bf16[8,1024,128]{1,2,0:T(8,128)(2,1)}, u32[]{:S(2)}, u32[]{:S(2)}) async-start(bf16[8,1024,128]{1,2,0:T(8,128)(2,1)} %broadcast_in_dim.4), calls=%async_computation.1 | async-start | bytes 4194304 | tf_op jit(solution)/shard_map/all_to_all | solution.py:14
  71.9 3.8 %copy.14 = bf16[8,128,64,1,16]{1,0,4,2,3:T(8,128)(2,1)} copy(bf16[8,128,64,1,16]{1,4,2,0,3:T(8,128)(2,1)S(1)} %bitcast.30) | data formatting | bytes 4194304 | tf_op jit(solution)/shard_map/all_to_all | solution.py:65
  75.7 33.4 %all-to-all-done.1 = bf16[8,1024,128]{1,2,0:T(8,128)(2,1)} async-done(((bf16[8,1024,128]{1,2,0:T(8,128)(2,1)}), bf16[8,1024,128]{1,2,0:T(8,128)(2,1)}, u32[]{:S(2)}, u32[]{:S(2)}) %all-to-all-start.1) | async-done | bytes 2097184 | tf_op jit(solution)/shard_map/all_to_all | solution.py:14
  109.1 4.6 %fusion.4 = bf16[1024,1024]{1,0:T(8,128)(2,1)S(1)} fusion(bf16[1024,1024]{0,1:T(8,128)(2,1)} %bitcast.5, bf16[128,8,8,128]{3,2,1,0:T(8,128)(2,1)} %bitcast.32), kind=kOutput, calls=%fused_computation.6 | convolution fusion | flops 2148532224 | bytes 6291456 | tf_op jit(solution)/shard_map/dot_general | solution.py:67
  113.7 75.6 %all_to_all.38 = bf16[64,16,1024]{2,1,0:T(8,128)(2,1)S(1)} all-to-all(bf16[64,16,1024]{2,1,0:T(8,128)(2,1)S(1)} %bitcast.33), channel_id=1, replica_groups=mesh['dp_0'=4,'dp_1'=8,'dp_2'=2,'tp_0'=4,'tp_1'=2] {'dp_0','dp_1','dp_2'}, dimensions={0} | all-to-all | bytes 4194304 | tf_op jit(solution)/shard_map/all_to_all | solution.py:36
  189.2 0.4 convert_reduce_fusion
  189.6 0.6 copy_bitcast_fusion
  190.2 6.9 %all-to-all-start.3 = ((f32[16,8,128]{2,0,1:T(8,128)}), f32[16,8,128]{2,0,1:T(8,128)S(1)}, u32[]{:S(2)}, u32[]{:S(2)}) async-start(f32[16,8,128]{2,0,1:T(8,128)} %copy_bitcast_fusion), calls=%async_computation.3 | async-start | bytes 131072 | tf_op jit(solution)/shard_map/all_to_all | solution.py:74
  197.1 0.7 multiply_reduce_fusion
  197.8 8.1 %psum.35 = f32[]{:T(128)} all-reduce(f32[]{:T(128)} %multiply_reduce_fusion), channel_id=1, replica_groups=mesh['dp_0'=4,'dp_1'=8,'dp_2'=2,'tp_0'=4,'tp_1'=2] {'dp_0'}, use_global_device_ids=true, to_apply=%region_2.0 | all-reduce | flops 1 | bytes 8 | tf_op jit(solution)/shard_map/psum | solution.py:42
  205.9 13.0 %psum.36 = f32[]{:T(128)} all-reduce(f32[]{:T(128)} %psum.35), channel_id=1, replica_groups=mesh['dp_0'=4,'dp_1'=8,'dp_2'=2,'tp_0'=4,'tp_1'=2] {'dp_1'}, use_global_device_ids=true, to_apply=%region_3.0 | all-reduce | flops 1 | bytes 8 | tf_op jit(solution)/shard_map/psum | solution.py:42
  218.9 4.8 %psum.37 = f32[]{:T(128)} all-reduce(f32[]{:T(128)} %psum.36), channel_id=1, replica_groups=mesh['dp_0'=4,'dp_1'=8,'dp_2'=2,'tp_0'=4,'tp_1'=2] {'dp_2'}, use_global_device_ids=true, to_apply=%region_4.0 | all-reduce | flops 1 | bytes 8 | tf_op jit(solution)/shard_map/psum | solution.py:42
  223.7 10.4 %psum.38 = f32[]{:T(128)} all-reduce(f32[]{:T(128)} %psum.37), channel_id=1, replica_groups=mesh['dp_0'=4,'dp_1'=8,'dp_2'=2,'tp_0'=4,'tp_1'=2] {'tp_0'}, use_global_device_ids=true, to_apply=%region_5.0 | all-reduce | flops 1 | bytes 8 | tf_op jit(solution)/shard_map/psum | solution.py:42
  234.0 12.0 %psum.39 = f32[]{:T(128)} all-reduce(f32[]{:T(128)} %psum.38), channel_id=1, replica_groups=mesh['dp_0'=4,'dp_1'=8,'dp_2'=2,'tp_0'=4,'tp_1'=2] {'tp_1'}, use_global_device_ids=true, to_apply=%region_6.0 | all-reduce | flops 1 | bytes 8 | tf_op jit(solution)/shard_map/psum | solution.py:42
  246.8 0.0 all-to-all-done.3
  246.8 0.6 broadcast_multiply_fusion
Async XLA Ops:
  6.1 10.5 %copy-start = (bf16[1024,128]{1,0:T(8,128)(2,1)S(1)}, bf16[1024,128]{1,0:T(8,128)(2,1)}, u32[]{:S(2)}) copy-start(bf16[1024,128]{1,0:T(8,128)(2,1)} %param.5) | copy-start | bytes 786436
  6.1 59.3 %all-to-all-start = ((bf16[128,64,8,16]{0,3,1,2:T(8,128)(2,1)}), bf16[128,64,8,16]{0,3,1,2:T(8,128)(2,1)S(1)}, u32[]{:S(2)}, u32[]{:S(2)}) async-start(bf16[128,64,8,16]{0,3,1,2:T(8,128)(2,1)} %copy.13), calls=%async_computation | async-start | bytes 4194304 | tf_op jit(solution)/shard_map/all_to_all | solution.py:65
  67.0 42.1 %all-to-all-start.1 = ((bf16[8,1024,128]{1,2,0:T(8,128)(2,1)}), bf16[8,1024,128]{1,2,0:T(8,128)(2,1)}, u32[]{:S(2)}, u32[]{:S(2)}) async-start(bf16[8,1024,128]{1,2,0:T(8,128)(2,1)} %broadcast_in_dim.4), calls=%async_computation.1 | async-start | bytes 4194304 | tf_op jit(solution)/shard_map/all_to_all | solution.py:14
  190.2 56.5 %all-to-all-start.3 = ((f32[16,8,128]{2,0,1:T(8,128)}), f32[16,8,128]{2,0,1:T(8,128)S(1)}, u32[]{:S(2)}, u32[]{:S(2)}) async-start(f32[16,8,128]{2,0,1:T(8,128)} %copy_bitcast_fusion), calls=%async_computation.3 | async-start | bytes 131072 | tf_op jit(solution)/shard_map/all_to_all | solution.py:74
where the time goes:
time: 248 us; the launch traced here: 247 us
  blocking collectives  124 us (50%)
  waiting for transfers between devices  82.1 us (33%)
  starting transfers between devices  22.3 us (9%)
  local copies, waits for them, and re-layouts  11.1 us (4%)
  matrix products  4.58 us (2%)
  other arithmetic  2.82 us (1%)
    all_to_all x1, blocking collectives, sent_and_summed(): lax.all_to_all(pieces, axis, split_axis=0, concat_axis=0, tiled=True)  75.6 us
    all_to_all x1, waiting for transfers between devices, body(): lax.all_to_all(inputs, TP, split_axis=2, concat_axis=0, tiled=True)  48.7 us
    psum x5, blocking collectives, over_axes(): shard = lax.psum(shard, axis)  48.2 us
    all_to_all x1, waiting for transfers between devices, copy_for_each(): return lax.all_to_all(copies, axis, split_axis=0, concat_axis=0, tiled=True)  33.4 us
    all_to_all x1, starting transfers between devices, body(): lax.all_to_all(inputs, TP, split_axis=2, concat_axis=0, tiled=True)  10.5 us
    all_to_all x1, starting transfers between devices, body(): local = lax.all_to_all(summed, TP, split_axis=1, concat_axis=0, tiled=True)  6.87 us
    all_to_all x1, starting transfers between devices, copy_for_each(): return lax.all_to_all(copies, axis, split_axis=0, concat_axis=0, tiled=True)  4.97 us
  transfers between devices with their start and end apart: 3, of which 2 were waited for; matrix products, arithmetic and copies ran while one was open for 2% of the time, Pallas kernels for 0%

commit v1 on v0

v1 whole, which is shorter than its diff:
```python
import jax
import jax.numpy as jnp
from jax import lax
from jax.experimental import pallas as pl
from jax.experimental.pallas import tpu as pltpu
from jax.sharding import Mesh
from jax.sharding import PartitionSpec as P

MESH = pl.DeviceIdType.MESH
NX, NZ, NH, NL, NC = 4, 8, 4, 2, 2
AXES = ("x", "z", "yl", "yh", "c")
HD = 128
TOK = 128
RX = 80
RZ = HD - RX
PHASES = NH
STAGES = 7
OFFSET = 2
NEWEST_FIRST = False
BF = jnp.bfloat16
F32 = jnp.float32


def mod(value, n):
    return lax.rem(value + 4 * n, n)


def kernel(
    x_hbm, s_ref, g_hbm, out_ref, ss_ref,
    xv, xd, xs, gb, gt, wx, wz,
    rxl, rxs, rzl, rzs, vz, vb, uz, ub,
    r2zl, r2zs, r2xl, r2xs, ty, ry, nsrc, n1, n2, n3,
    ld_sem, g_ss, g_rs, xo_ss, xo_rs, xp_ss, xp_rs, xf_ss, xf_rs,
    xl_ss, xl_rs, xq_ss, xq_rs, zl_ss, zl_rs, zs_ss, zs_rs,
    z2l_ss, z2l_rs, z2s_ss, z2s_rs, x2l_ss, x2l_rs, x2s_ss, x2s_rs,
    y_ss, y_rs, n1_ss, n1_rs, n2_ss, n2_rs, n3_ss, n3_rs,
):
    x, z, yl, yh, c = (lax.axis_index(name) for name in AXES)
    quarter = NZ * 2 * HD

    def push(src, dst, ss, rs, dev):
        pltpu.make_async_remote_copy(
            src_ref=src, dst_ref=dst, send_sem=ss, recv_sem=rs, device_id=dev, device_id_type=MESH
        ).start()

    def arrived(dst, rs):
        pltpu.make_async_remote_copy(
            src_ref=dst, dst_ref=dst, send_sem=rs, recv_sem=rs, device_id={"c": 1 - c}, device_id_type=MESH
        ).wait_recv()

    def sent(src, ss):
        pltpu.make_async_remote_copy(
            src_ref=src, dst_ref=src, send_sem=ss, recv_sem=ss, device_id={"c": 1 - c}, device_id_type=MESH
        ).wait_send()

    def order_x(i):
        return mod(x + jnp.where(i == 0, 2, jnp.where(i == 1, 1, jnp.where(i == 2, 3, 0))), NX)

    def load(i):
        xq = order_x(i)
        cols = pl.ds(pl.multiple_of(xq * quarter, quarter), quarter)
        return pltpu.make_async_copy(x_hbm.at[:, cols], xv.at[:, cols], ld_sem.at[i])

    for i in range(NX):
        load(i).start()
    own_g = pltpu.make_async_copy(g_hbm.at[pl.ds(pl.multiple_of(yh * 256, 256), 256), :], gb.at[0, 0], ld_sem.at[NX])
    own_g.start()

    barrier = pltpu.get_barrier_semaphore()

    def greet(dev):
        pl.semaphore_signal(barrier, inc=1, device_id=dev, device_id_type=MESH)

    y_line = [(a, b, e) for a in range(NH) for b in range(NL) for e in range(NC) if (a, b, e) != (0, 0, 0)]

    def y_dev(a, b, e):
        return {"yh": mod(yh + a, NH), "yl": mod(yl + b, NL), "c": mod(c + e, NC)}

    for k in range(1, NX):
        greet({"x": mod(x + k, NX)})
    for k in range(1, NZ):
        greet({"z": mod(z + k, NZ)})
    for a, b, e in y_line:
        greet(y_dev(a, b, e))
    pl.semaphore_wait(barrier, NX - 1 + NZ - 1 + len(y_line))

    def slab(k):
        return g_hbm.at[pl.ds(pl.multiple_of(mod(k, NH) * 256, 256), 256), :]

    def send_g(p, first=False):
        user = mod(yh - p, NH)
        if not first:
            push(slab(user), gb.at[p, 0], g_ss.at[p, 0], g_rs.at[p, 0], {"yh": user})
        other = {"yh": user, "yl": 1 - yl}
        push(slab(user), gb.at[p, 1], g_ss.at[p, 1], g_rs.at[p, 1], other)
        push(slab(user + 1 - 2 * yl), gb.at[p, 2], g_ss.at[p, 2], g_rs.at[p, 2], other)

    send_g(0, True)

    scales = s_ref[...].astype(F32).T.astype(BF)
    blocks = scales.shape[1]

    def dequant(b):
        pick = (lax.broadcasted_iota(jnp.int32, (blocks, HD), 0) == b).astype(F32).astype(BF)
        spread = jnp.dot(scales, pick, preferred_element_type=F32)
        v = xv[:, pl.ds(pl.multiple_of(b * HD, HD), HD)].astype(F32)
        return (v * spread).astype(BF)

    @pl.loop(0, NX)
    def _(i):
        xq = order_x(i)
        load(i).wait()

        @pl.loop(0, NZ)
        def _(zq):
            par, j = lax.rem(zq, 2), zq // 2
            s = lax.rem(zq + yl, 2)
            b = (xq * NZ + zq) * 2
            xd[c, xq, par, j] = dequant(b + s)
            xs[xq, par, j] = dequant(b + 1 - s)

        push(xd.at[c, xq], xd.at[c, xq], xo_ss.at[xq], xo_rs.at[xq], {"c": 1 - c})
        for par in range(2):
            s_out = lax.rem(par + yl + 1, 2)
            partner = {"yh": mod(yh + s_out * (2 * yl - 1), NH), "yl": 1 - yl}
            push(xs.at[xq, par], xd.at[2 + c, xq, par], xp_ss.at[xq, par], xp_rs.at[xq, par], partner)

    def pass_on(i):
        xq = order_x(i)
        for par in range(2):
            arrived(xd.at[2 + c, xq, par], xp_rs.at[xq, par])
        push(xd.at[2 + c, xq], xd.at[2 + c, xq], xf_ss.at[xq], xf_rs.at[xq], {"c": 1 - c})

    def product(p, xq):
        for par in range(2):
            s = lax.rem(par + yl, 2)
            lhs = jnp.concatenate([gt[0], gt[1 + s]], axis=1)
            for jj in range(2):
                rhs = jnp.concatenate(
                    [
                        jnp.concatenate([xd[k, xq, par, 2 * jj + e] for k in range(4)], axis=0)
                        for e in range(2)
                    ],
                    axis=1,
                )
                res = jnp.dot(lhs, rhs, preferred_element_type=F32).astype(BF)
                for e in range(2):
                    j = 2 * jj + e
                    wx[p, xq, par, j] = res[:RX, e * HD : (e + 1) * HD]
                    wz[p, 2 * j + par, xq] = res[RX:, e * HD : (e + 1) * HD]

    def xdir(par):
        return 1 - 2 * par

    def stage0(p):
        @pl.when(p == 0)
        def _():
            own_g.wait()

        @pl.when(p > 0)
        def _():
            arrived(gb.at[p, 0], g_rs.at[p, 0])

        for k in range(1, 3):
            arrived(gb.at[p, k], g_rs.at[p, k])
        for k in range(3):
            gt[k] = gb[p, k].astype(F32).T.astype(BF)

        @pl.when(p == 0)
        def _():
            pass_on(0)

        @pl.loop(0, NX)
        def _(i):
            xq = order_x(i)

            @pl.when(p == 0)
            def _():
                @pl.when(i < NX - 1)
                def _():
                    pass_on(i + 1)

                arrived(xd.at[1 - c, xq], xo_rs.at[xq])
                arrived(xd.at[3 - c, xq], xf_rs.at[xq])

            product(p, xq)

            @pl.when(i == 0)
            def _():
                for par in range(2):
                    d = xdir(par)
                    push(wx.at[p, xq, par], rxl.at[p, 0, par], xl_ss.at[p, 0, par], xl_rs.at[p, 0, par], {"x": mod(x + d, NX)})

            @pl.when(i == 1)
            def _():
                push(wx.at[p, xq, 1], rxs.at[p, 1], xq_ss.at[p, 1], xq_rs.at[p, 1], {"x": xq})

            @pl.when(i == 2)
            def _():
                push(wx.at[p, xq, 0], rxs.at[p, 0], xq_ss.at[p, 0], xq_rs.at[p, 0], {"x": xq})

            @pl.when((i == 1) & (p < PHASES - 1))
            def _():
                send_g(p + 1)

        for h in range(2):
            z_long(p, 0, h)
            z_short(p, 0, h)

    def z_long(p, k, h):
        d = xdir(h)
        push(
            wz.at[p, mod(z + (4 - k) * d, NZ), pl.ds(2 * h, 2)], rzl.at[p, k, h],
            zl_ss.at[p, k, h], zl_rs.at[p, k, h], {"z": mod(z + d, NZ)},
        )

    def z_short(p, k, h):
        d = xdir(h)
        push(
            wz.at[p, mod(z - (3 - k) * d, NZ), pl.ds(2 * h, 2)], rzs.at[p, k, h],
            zs_ss.at[p, k, h], zs_rs.at[p, k, h], {"z": mod(z - d, NZ)},
        )

    def z_long_add(p, k, h):
        t = mod(z + (3 - k) * xdir(h), NZ)
        arrived(rzl.at[p, k, h], zl_rs.at[p, k, h])
        for e in range(2):
            wz[p, t, 2 * h + e] = (wz[p, t, 2 * h + e].astype(F32) + rzl[p, k, h, e].astype(F32)).astype(BF)
        z_long(p, k + 1, h)

    def z_short_add(p, k, h):
        t = mod(z - (2 - k) * xdir(h), NZ)
        arrived(rzs.at[p, k, h], zs_rs.at[p, k, h])
        for e in range(2):
            wz[p, t, 2 * h + e] = (wz[p, t, 2 * h + e].astype(F32) + rzs[p, k, h, e].astype(F32)).astype(BF)
        z_short(p, k + 1, h)

    def pdir(p):
        return 1 - 2 * lax.rem(p, 2)

    def z2_long(p, k, t):
        push(
            vb.at[p, t], r2zl.at[p, k], z2l_ss.at[p, k], z2l_rs.at[p, k], {"z": mod(z + pdir(p), NZ)}
        )

    def z2_short(p, k, t):
        push(
            vb.at[p, t], r2zs.at[p, k], z2s_ss.at[p, k], z2s_rs.at[p, k], {"z": mod(z - pdir(p), NZ)}
        )

    def z2_long_add(p, k):
        t = mod(z + (3 - k) * pdir(p), NZ)
        arrived(r2zl.at[p, k], z2l_rs.at[p, k])
        vb[p, t] = (vz[p, t] + r2zl[p, k].astype(F32)).astype(BF)
        z2_long(p, k + 1, t)

    def z2_short_add(p, k):
        t = mod(z - (2 - k) * pdir(p), NZ)
        arrived(r2zs.at[p, k], z2s_rs.at[p, k])
        vb[p, t] = (vz[p, t] + r2zs[p, k].astype(F32)).astype(BF)
        z2_short(p, k + 1, t)

    def stage1(p):
        for par in range(2):
            d = xdir(par)
            t = mod(x + d, NX)
            arrived(rxl.at[p, 0, par], xl_rs.at[p, 0, par])
            for j in range(4):
                wx[p, t, par, j] = (wx[p, t, par, j].astype(F32) + rxl[p, 0, par, j].astype(F32)).astype(BF)
            push(wx.at[p, t, par], rxl.at[p, 1, par], xl_ss.at[p, 1, par], xl_rs.at[p, 1, par], {"x": t})
        for h in range(2):
            z_long_add(p, 0, h)
            z_short_add(p, 0, h)

    def stage2(p):
        for par in range(2):
            arrived(rxs.at[p, par], xq_rs.at[p, par])
            arrived(rxl.at[p, 1, par], xl_rs.at[p, 1, par])
            for j in range(4):
                vz[p, 2 * j + par] = (
                    wx[p, x, par, j].astype(F32) + rxs[p, par, j].astype(F32) + rxl[p, 1, par, j].astype(F32)
                )
        d = pdir(p)
        t = mod(z + 4 * d, NZ)
        vb[p, t] = vz[p, t].astype(BF)
        z2_long(p, 0, t)
        t = mod(z - 3 * d, NZ)
        vb[p, t] = vz[p, t].astype(BF)
        z2_short(p, 0, t)
        for h in range(2):
            z_long_add(p, 1, h)
            z_short_add(p, 1, h)

    def stage3(p):
        for h in range(2):
            z_long_add(p, 2, h)
        z2_long_add(p, 0)
        z2_short_add(p, 0)

    def stage4(p):
        for h in range(2):
            arrived(rzs.at[p, 2, h], zs_rs.at[p, 2, h])
            arrived(rzl.at[p, 3, h], zl_rs.at[p, 3, h])
            for e in range(2):
                uz[p, 2 * h + e] = (
                    wz[p, z, 2 * h + e].astype(F32) + rzs[p, 2, h, e].astype(F32) + rzl[p, 3, h, e].astype(F32)
                )
        d = pdir(p)
        t = mod(x + 2 * d, NX)
        ub[p, t] = uz[p, t].astype(BF)
        push(ub.at[p, t], r2xl.at[p, 0], x2l_ss.at[p, 0], x2l_rs.at[p, 0], {"x": mod(x + d, NX)})
        t = mod(x - d, NX)
        ub[p, t] = uz[p, t].astype(BF)
        push(ub.at[p, t], r2xs.at[p], x2s_ss.at[p], x2s_rs.at[p], {"x": t})
        z2_long_add(p, 1)
        z2_short_add(p, 1)

    def stage5(p):
        t = mod(x + pdir(p), NX)
        arrived(r2xl.at[p, 0], x2l_rs.at[p, 0])
        ub[p, t] = (uz[p, t] + r2xl[p, 0].astype(F32)).astype(BF)
        push(ub.at[p, t], r2xl.at[p, 1], x2l_ss.at[p, 1], x2l_rs.at[p, 1], {"x": t})
        z2_long_add(p, 2)

    s_mine = lax.rem(z + yl, 2)
    stays = s_mine == yl

    def stage6(p):
        arrived(r2xs.at[p], x2s_rs.at[p])
        arrived(r2xl.at[p, 1], x2l_rs.at[p, 1])
        arrived(r2zs.at[p, 2], z2s_rs.at[p, 2])
        arrived(r2zl.at[p, 3], z2l_rs.at[p, 3])
        ty[p, :RX] = vz[p, z] + r2zs[p, 2].astype(F32) + r2zl[p, 3].astype(F32)
        ty[p, RX:] = uz[p, x] + r2xs[p].astype(F32) + r2xl[p, 1].astype(F32)
        local = (p == 0) & stays

        @pl.when(local)
        def _():
            ry[0] = ty[0]

        @pl.when(jnp.logical_not(local))
        def _():
            push(ty.at[p], ry.at[p], y_ss.at[p], y_rs.at[p], {"yh": mod(yh + p, NH), "yl": s_mine})

    stages = [stage0, stage1, stage2, stage3, stage4, stage5, stage6]

    @pl.loop(0, STAGES + OFFSET * (PHASES - 1))
    def _(t):
        order = range(STAGES) if NEWEST_FIRST else range(STAGES - 1, -1, -1)
        for k in order:
            ahead = t - k + 8 * OFFSET
            p = ahead // OFFSET - 8

            @pl.when((lax.rem(ahead, OFFSET) == 0) & (p >= 0) & (p < PHASES))
            def _():
                stages[k](p)

    for p in range(1, PHASES):
        arrived(ry.at[p], y_rs.at[p])

    @pl.when(jnp.logical_not(stays))
    def _():
        arrived(ry.at[0], y_rs.at[0])

    total = ry[0] + ry[1] + ry[2] + ry[3]
    out_ref[...] = total.T

    part = jnp.sum((total * total).reshape(16, 8, HD), axis=0)
    nsrc[0] = part
    for k in range(1, NX):
        t = mod(x + k, NX)
        push(nsrc.at[0], n1.at[x], n1_ss.at[t], n1_rs.at[x], {"x": t})
    n1[x] = part
    for k in range(1, NX):
        t = mod(x + k, NX)
        arrived(n1.at[t], n1_rs.at[t])
    part = jnp.sum(n1[...], axis=0)
    nsrc[1] = part
    for k in range(1, NZ):
        t = mod(z + k, NZ)
        push(nsrc.at[1], n2.at[z], n2_ss.at[t], n2_rs.at[z], {"z": t})
    n2[z] = part
    for k in range(1, NZ):
        t = mod(z + k, NZ)
        arrived(n2.at[t], n2_rs.at[t])
    part = jnp.sum(n2[...], axis=0)
    nsrc[2] = part

    def place(h, l, e):
        return (h * NL + l) * NC + e

    mine = place(yh, yl, c)
    for a, b, e in y_line:
        dev = y_dev(a, b, e)
        t = place(dev["yh"], dev["yl"], dev["c"])
        push(nsrc.at[2], n3.at[mine], n3_ss.at[t], n3_rs.at[mine], dev)
    n3[mine] = part
    for a, b, e in y_line:
        dev = y_dev(a, b, e)
        t = place(dev["yh"], dev["yl"], dev["c"])
        arrived(n3.at[t], n3_rs.at[t])
    part = jnp.sum(n3[...], axis=0)
    whole = jnp.sum(jnp.sum(part, axis=1, keepdims=True), axis=0, keepdims=True)
    ss_ref[...] = jnp.broadcast_to(whole, (8, HD))

    for k in range(1, NX):
        t = mod(x + k, NX)
        sent(nsrc.at[0], n1_ss.at[t])
    for k in range(1, NZ):
        t = mod(z + k, NZ)
        sent(nsrc.at[1], n2_ss.at[t])
    for a, b, e in y_line:
        dev = y_dev(a, b, e)
        sent(nsrc.at[2], n3_ss.at[place(dev["yh"], dev["yl"], dev["c"])])

    @pl.when(jnp.logical_not(stays))
    def _():
        sent(ty.at[0], y_ss.at[0])

    @pl.loop(0, PHASES)
    def _(p):
        @pl.when(p > 0)
        def _():
            sent(ty.at[p], y_ss.at[p])
            sent(gb.at[p, 0], g_ss.at[p, 0])

        sent(gb.at[p, 1], g_ss.at[p, 1])
        sent(gb.at[p, 2], g_ss.at[p, 2])
        for h in range(2):
            for k in range(2):
                sent(rxl.at[p, k, h], xl_ss.at[p, k, h])
            sent(rxs.at[p, h], xq_ss.at[p, h])
            for k in range(4):
                sent(rzl.at[p, k, h], zl_ss.at[p, k, h])
            for k in range(3):
                sent(rzs.at[p, k, h], zs_ss.at[p, k, h])
        for k in range(4):
            sent(r2zl.at[p, k], z2l_ss.at[p, k])
        for k in range(3):
            sent(r2zs.at[p, k], z2s_ss.at[p, k])
        for k in range(2):
            sent(r2xl.at[p, k], x2l_ss.at[p, k])
        sent(r2xs.at[p], x2s_ss.at[p])

    @pl.loop(0, NX)
    def _(q):
        sent(xd.at[c, q], xo_ss.at[q])
        sent(xd.at[2 + c, q], xf_ss.at[q])
        for par in range(2):
            sent(xs.at[q, par], xp_ss.at[q, par])


def body(stash_values, stash_scales, value_grad):
    tokens, width = stash_values.shape
    blocks = stash_scales.shape[1]
    dma = pltpu.SemaphoreType.DMA
    pairs = [
        (PHASES, 3), (NX,), (NX, 2), (NX,),
        (PHASES, 2, 2), (PHASES, 2), (PHASES, 4, 2), (PHASES, 3, 2),
        (PHASES, 4), (PHASES, 3), (PHASES, 2), (PHASES,),
        (PHASES,), (NX,), (NZ,), (NH * NL * NC,),
    ]
    total, square = pl.pallas_call(
        kernel,
        out_shape=(
            jax.ShapeDtypeStruct((HD, HD), F32),
            jax.ShapeDtypeStruct((8, HD), F32),
        ),
        in_specs=[
            pl.BlockSpec(memory_space=pl.ANY),
            pl.BlockSpec(memory_space=pltpu.VMEM),
            pl.BlockSpec(memory_space=pl.ANY),
        ],
        out_specs=(
            pl.BlockSpec(memory_space=pltpu.VMEM),
            pl.BlockSpec(memory_space=pltpu.VMEM),
        ),
        scratch_shapes=[
            pltpu.VMEM((tokens, width), BF),
            pltpu.VMEM((4, NX, 2, 4, TOK, HD), BF),
            pltpu.VMEM((NX, 2, 4, TOK, HD), BF),
            pltpu.VMEM((PHASES, 3, 2 * TOK, HD), BF),
            pltpu.VMEM((3, HD, 2 * TOK), BF),
            pltpu.VMEM((PHASES, NX, 2, 4, RX, HD), BF),
            pltpu.VMEM((PHASES, NZ, NX, RZ, HD), BF),
            pltpu.VMEM((PHASES, 2, 2, 4, RX, HD), BF),
            pltpu.VMEM((PHASES, 2, 4, RX, HD), BF),
            pltpu.VMEM((PHASES, 4, 2, 2, RZ, HD), BF),
            pltpu.VMEM((PHASES, 3, 2, 2, RZ, HD), BF),
            pltpu.VMEM((PHASES, NZ, RX, HD), F32),
            pltpu.VMEM((PHASES, NZ, RX, HD), BF),
            pltpu.VMEM((PHASES, NX, RZ, HD), F32),
            pltpu.VMEM((PHASES, NX, RZ, HD), BF),
            pltpu.VMEM((PHASES, 4, RX, HD), BF),
            pltpu.VMEM((PHASES, 3, RX, HD), BF),
            pltpu.VMEM((PHASES, 2, RZ, HD), BF),
            pltpu.VMEM((PHASES, RZ, HD), BF),
            pltpu.VMEM((PHASES, HD, HD), F32),
            pltpu.VMEM((PHASES, HD, HD), F32),
            pltpu.VMEM((3, 8, HD), F32),
            pltpu.VMEM((NX, 8, HD), F32),
            pltpu.VMEM((NZ, 8, HD), F32),
            pltpu.VMEM((NH * NL * NC, 8, HD), F32),
            dma((NX + 1,)),
            *(dma(shape) for pair in pairs for shape in (pair, pair)),
        ],
        compiler_params=pltpu.CompilerParams(
            collective_id=0, has_side_effects=True, vmem_limit_bytes=56 * 1024 * 1024
        ),
    )(stash_values, stash_scales.T, value_grad)
    limit = jnp.sqrt(jnp.float32(width * HD * lax.axis_size("yh") * lax.axis_size("c")))
    return total * jnp.minimum(jnp.float32(1.0), limit / jnp.sqrt(square[0, 0]))


def solution(mesh):
    torus = Mesh(mesh.devices.reshape(NX, NZ, NL, NH, NC), AXES)
    rows = ("x", "z", "yl", "yh", "c")
    return jax.shard_map(
        body,
        mesh=torus,
        in_specs=(P(rows, None), P(rows, None), P(("x", "z", "yl"), ("yh", "c"))),
        out_specs=P(("x", "z", "yl"), ("yh", "c")),
        check_vma=False,
    )
```

time: 248 us -> 113 us (0.46)
  blocking collectives: 124 us -> 0 us
  Pallas kernels: 0 us -> 110 us
  waiting for transfers between devices: 82.1 us -> 0 us
  starting transfers between devices: 22.3 us -> 0 us
  local copies, waits for them, and re-layouts: 11.1 us -> 1.19 us
  matrix products: 4.58 us -> 0 us
    pallas_call x0 -> x1, Pallas kernels: none -> 110 us  [body(): pl.pallas_call(kernel, out_shape=(jax.ShapeDtypeStruct((HD, HD), F32), ja...]
    all_to_all x3 -> x0, waiting for transfers between devices: 82.1 us -> none  [the longest x1 48.7 us: body(): lax.all_to_all(inputs, TP, split_axis=2, concat_axis=0, tiled=True)]
    all_to_all x1 -> x0, blocking collectives: 75.6 us -> none  [sent_and_summed(): lax.all_to_all(pieces, axis, split_axis=0, concat_axis=0, tiled=True)]
    psum x5 -> x0, blocking collectives: 48.2 us -> none  [over_axes(): shard = lax.psum(shard, axis)]
    all_to_all x3 -> x0, starting transfers between devices: 22.3 us -> none  [the longest x1 10.5 us: body(): lax.all_to_all(inputs, TP, split_axis=2, concat_axis=0, tiled=True)]
    dot_general x1 -> x0, matrix products: 4.58 us -> none  [body(): lax.dot_general(features, collect(value_grad, TP, 1), (((0,), (0,)), ((),...]
    all_to_all x2 -> x0, local copies, waits for them, and re-layouts: 4.4 us -> none  [the longest x1 3.76 us: body(): lax.all_to_all(inputs, TP, split_axis=2, concat_axis=0, tiled=True)]
    unnamed x4 -> x0, local copies, waits for them, and re-layouts: 3.36 us -> none
  transfers between devices with their start and end apart: 3 -> 0, of which waited for: 2 -> 0; matrix products, arithmetic and copies ran while one was open for 2% -> 0% of each run, Pallas kernels for 0% -> 0%
where the time goes in v1:
time: 113 us
  Pallas kernels  110 us (97%)
  other arithmetic  1.48 us (1%)
  local copies, waits for them, and re-layouts  1.19 us (1%)
    pallas_call x1, Pallas kernels, body(): pl.pallas_call(kernel, out_shape=(jax.ShapeDtypeStruct((HD, HD), F32), ja...  110 us

profile of v1, /device:TPU:1, one launch (start us, length us, event | category | flops | bytes accessed | tf_op | source)
XLA Modules:
  0.0 112.9 jit_solution(14524978371383157495)
XLA Ops:
  0.0 109.5 %shard_map.37 = (f32[128,128]{1,0:T(8,128)}, f32[8,128]{1,0:T(8,128)}) custom-call(bf16[128,8192]{1,0:T(8,128)(2,1)} %x_hbm.1, bf16[64,128]{1,0:T(8,128)(2,1)} %bitcast.2, bf16[1024,128]{1,0:T(8,128)(2,1)} %g_hbm.1), custom_call_target="tpu_custom_call" | custom-call | tf_op jit(solution)/shard_map/pallas_call | solution.py:463
  109.5 1.2 %slice.3 = f32[1,1]{1,0:T(1,128)} slice(f32[8,128]{1,0:T(8,128)} %get-tuple-element.8), slice={[0:1], [0:1]} | slice | bytes 8 | tf_op jit(solution)/shard_map/slice | solution.py:512
  111.4 1.5 %broadcast_multiply_fusion = f32[128,128]{1,0:T(8,128)} fusion(f32[128,128]{1,0:T(8,128)} %get-tuple-element.7, f32[]{:T(128)} %bitcast.1), kind=kLoop, calls=%fused_computation | loop fusion | flops 16384 | bytes 131076 | tf_op jit(solution)/shard_map/mul | solution.py:512

commit v2 on v1

v2 whole, which is shorter than its diff:
```python
import functools
import math

import jax
import jax.numpy as jnp
from jax import lax
from jax.experimental import pallas as pl
from jax.experimental.pallas import tpu as pltpu
from jax.sharding import Mesh
from jax.sharding import PartitionSpec as P

MESH = pl.DeviceIdType.MESH
NX, NZ, NH, NL, NC = 4, 8, 4, 2, 2
AXES = ("x", "z", "yl", "yh", "c")
HD = 128
TOK = 128
RX = 80
RZ = HD - RX
PHASES = NH
SEQUENCE = (
    ("M", 0, 0), ("M", 0, 1), ("xa", 0, 0), ("M", 0, 2), ("xa", 0, 1), ("M", 0, 3), ("G", 1), ("G", 3), ("zl", 0, 0, 0),
    ("zs", 0, 0, 0), ("xb", 0), ("zl", 0, 0, 1), ("zs", 0, 0, 1), ("N", 1), ("G", 2), ("z2l", 0, 0), ("z2s", 0, 0),
    ("zl", 0, 1, 0), ("zs", 0, 1, 0), ("zs", 0, 1, 1), ("zl", 0, 1, 1), ("N", 2), ("z2l", 0, 1), ("z2s", 0, 1),
    ("zl", 0, 2, 0), ("xa", 1, 0), ("xa", 1, 1), ("zl", 1, 0, 0), ("zl", 0, 2, 1), ("zs", 1, 0, 0), ("zl", 1, 0, 1),
    ("zs", 1, 0, 1), ("N", 3), ("z2l", 0, 2), ("zb", 0), ("xa", 2, 0), ("xa", 2, 1), ("zl", 2, 0, 0),
    ("zl", 1, 1, 0), ("zs", 1, 1, 0), ("zs", 2, 0, 0), ("zl", 2, 0, 1), ("zs", 2, 0, 1), ("zl", 1, 1, 1),
    ("zs", 1, 1, 1), ("zl", 3, 0, 0), ("zs", 3, 0, 0), ("zl", 3, 0, 1), ("zs", 3, 0, 1), ("xb", 1), ("zl", 2, 1, 0),
    ("zs", 2, 1, 0), ("zl", 1, 2, 0), ("zl", 2, 1, 1), ("zs", 2, 1, 1), ("zl", 1, 2, 1), ("xa", 3, 0), ("xa", 3, 1),
    ("zs", 3, 1, 0), ("zl", 3, 1, 0), ("zl", 3, 1, 1), ("z2l", 1, 0), ("zs", 3, 1, 1), ("z2s", 1, 0), ("x2a", 0),
    ("zl", 2, 2, 0), ("zl", 2, 2, 1), ("zb", 1), ("xb", 2), ("zl", 3, 2, 0), ("zl", 3, 2, 1), ("z2l", 1, 1),
    ("z2s", 1, 1), ("zb", 2), ("xb", 3), ("f", 0), ("x2a", 1), ("z2l", 2, 0), ("z2s", 2, 0), ("zb", 3),
    ("z2l", 1, 2), ("x2a", 2), ("z2l", 3, 0), ("z2s", 3, 0), ("z2l", 2, 1), ("z2s", 2, 1), ("x2a", 3), ("f", 1),
    ("z2l", 3, 1), ("z2s", 3, 1), ("z2l", 2, 2), ("z2l", 3, 2), ("f", 2), ("f", 3),
)
BF = jnp.bfloat16
F32 = jnp.float32


def mod(value, n):
    return lax.rem(value + 4 * n, n)


def kernel(
    limit, x_hbm, s_hbm, g_hbm, out_ref,
    xv, sv, xd, xs, gb, gt, wx, wz,
    rxl, rxs, rzl, rzs, vz, vb, uz, ub,
    r2zl, r2zs, r2xl, r2xs, ty, ry, nsrc, n1, n2, n3,
    ld_sem, g_ss, g_rs, xo_ss, xo_rs, xp_ss, xp_rs, xf_ss, xf_rs,
    xl_ss, xl_rs, xq_ss, xq_rs, zl_ss, zl_rs, zs_ss, zs_rs,
    z2l_ss, z2l_rs, z2s_ss, z2s_rs, x2l_ss, x2l_rs, x2s_ss, x2s_rs,
    y_ss, y_rs, n1_ss, n1_rs, n2_ss, n2_rs, n3_ss, n3_rs,
):
    x, z, yl, yh, c = (lax.axis_index(name) for name in AXES)
    quarter = NZ * 2 * HD

    def push(src, dst, ss, rs, dev):
        pltpu.make_async_remote_copy(
            src_ref=src, dst_ref=dst, send_sem=ss, recv_sem=rs, device_id=dev, device_id_type=MESH
        ).start()

    def arrived(dst, rs):
        pltpu.make_async_remote_copy(
            src_ref=dst, dst_ref=dst, send_sem=rs, recv_sem=rs, device_id={"c": 1 - c}, device_id_type=MESH
        ).wait_recv()

    def sent(src, ss):
        pltpu.make_async_remote_copy(
            src_ref=src, dst_ref=src, send_sem=ss, recv_sem=ss, device_id={"c": 1 - c}, device_id_type=MESH
        ).wait_send()

    def order_x(i):
        if isinstance(i, int):
            return mod(x + (2, 1, 3, 0)[i], NX)
        return mod(x + jnp.where(i == 0, 2, jnp.where(i == 1, 1, jnp.where(i == 2, 3, 0))), NX)

    def load(i):
        xq = order_x(i)
        cols = pl.ds(pl.multiple_of(xq * quarter, quarter), quarter)
        return pltpu.make_async_copy(x_hbm.at[:, cols], xv.at[:, cols], ld_sem.at[i])

    load(0).start()
    own_g = pltpu.make_async_copy(g_hbm.at[pl.ds(pl.multiple_of(yh * 256, 256), 256), :], gb.at[0, 0], ld_sem.at[NX])
    scale_load = pltpu.make_async_copy(s_hbm, sv, ld_sem.at[NX + 1])
    scale_load.start()

    barrier = pltpu.get_barrier_semaphore()

    def greet(dev):
        pl.semaphore_signal(barrier, inc=1, device_id=dev, device_id_type=MESH)

    x_line = [(k, e) for k in range(NX) for e in range(NC) if (k, e) != (0, 0)]
    y_line = [(a, b) for a in range(NH) for b in range(NL) if (a, b) != (0, 0)]

    def x_dev(k, e):
        return {"x": mod(x + k, NX), "c": mod(c + e, NC)}

    def y_dev(a, b):
        return {"yh": mod(yh + a, NH), "yl": mod(yl + b, NL)}

    for k, e in x_line:
        greet(x_dev(k, e))
    for k in range(1, NZ):
        greet({"z": mod(z + k, NZ)})
    for a, b in y_line:
        greet(y_dev(a, b))

    for i in range(1, NX):
        load(i).start()
    own_g.start()

    def slab(k):
        return g_hbm.at[pl.ds(pl.multiple_of(mod(k, NH) * 256, 256), 256), :]

    beside = {"yl": 1 - yl}
    beyond = {"yh": mod(yh + 2 * yl - 1, NH), "yl": 1 - yl}

    def offset(p):
        if p % 2 == 0:
            return p
        return jnp.where(yl == 1, p, NH - p)

    def send_first_g():
        push(slab(yh), gb.at[0, 1], g_ss.at[0, 1], g_rs.at[0, 1], beside)
        push(slab(yh + 1 - 2 * yl), gb.at[0, 2], g_ss.at[0, 3], g_rs.at[0, 2], beside)

    def send_g(o):
        if o == 0:
            push(slab(yh), gb.at[1 + 2 * yl, 2], g_ss.at[0, 2], g_rs.at[1 + 2 * yl, 2], beyond)
        else:
            user = mod(yh - o, NH)
            push(slab(user), gb.at[o, 0], g_ss.at[o, 0], g_rs.at[o, 0], {"yh": user})

    def op_g(o):
        arrived(gb.at[o, 0], g_rs.at[o, 0])
        push(gb.at[o, 0], gb.at[o, 1], g_ss.at[o, 1], g_rs.at[o, 1], beside)
        other = mod(o + 1 - 2 * yl, NH)

        @pl.when(other > 0)
        def _():
            push(gb.at[o, 0], gb.at[other, 2], g_ss.at[o, 2], g_rs.at[other, 2], beyond)

    scale_load.wait()
    scales = sv[...].astype(F32).T.astype(BF)
    blocks = scales.shape[1]

    def dequant(b):
        pick = (lax.broadcasted_iota(jnp.int32, (blocks, HD), 0) == b).astype(F32).astype(BF)
        spread = jnp.dot(scales, pick, preferred_element_type=F32)
        v = xv[:, pl.ds(pl.multiple_of(b * HD, HD), HD)].astype(F32)
        return (v * spread).astype(BF)

    def prepare(i):
        xq = order_x(i)
        load(i).wait()

        @pl.loop(0, NZ, unroll=4)
        def _(zq):
            par, j = lax.rem(zq, 2), zq // 2
            s = lax.rem(zq + yl, 2)
            b = (xq * NZ + zq) * 2
            xs[xq, par, j] = dequant(b + 1 - s)
            xd[c, xq, par, j] = dequant(b + s)

    def share(i):
        xq = order_x(i)
        for par in range(2):
            s_out = lax.rem(par + yl + 1, 2)
            partner = {"yh": mod(yh + s_out * (2 * yl - 1), NH), "yl": 1 - yl}
            push(xs.at[xq, par], xd.at[2 + c, xq, par], xp_ss.at[xq, par], xp_rs.at[xq, par], partner)
        push(xd.at[c, xq], xd.at[c, xq], xo_ss.at[xq], xo_rs.at[xq], {"c": 1 - c})

    prepare(0)
    pl.semaphore_wait(barrier, len(x_line) + NZ - 1 + len(y_line))
    share(0)
    send_first_g()

    @pl.loop(1, NX)
    def _(i):
        prepare(i)
        share(i)

    near = lax.rem(yl + 1, 2)

    def pass_on(i):
        xq = order_x(i)
        for k in range(2):
            par = lax.rem(near + k, 2)
            arrived(xd.at[2 + c, xq, par], xp_rs.at[xq, par])
            push(xd.at[2 + c, xq, par], xd.at[2 + c, xq, par], xf_ss.at[xq, par], xf_rs.at[xq, par], {"c": 1 - c})

    def product(p, xq):
        for par in range(2):
            s = lax.rem(par + yl, 2)
            lhs = jnp.concatenate([gt[0], gt[1 + s]], axis=1)
            for jj in range(2):
                rhs = jnp.concatenate(
                    [
                        jnp.concatenate([xd[k, xq, par, 2 * jj + e] for k in range(4)], axis=0)
                        for e in range(2)
                    ],
                    axis=1,
                )
                res = jnp.dot(lhs, rhs, preferred_element_type=F32).astype(BF)
                for e in range(2):
                    j = 2 * jj + e
                    wx[p, xq, par, j] = res[:RX, e * HD : (e + 1) * HD]
                    wz[p, 2 * j + par, xq] = res[RX:, e * HD : (e + 1) * HD]

    def xdir(par):
        return 1 - 2 * par

    def after_product(p, i, xq):
        def when(k, run):
            if isinstance(i, int):
                if i == k:
                    run()
            else:
                pl.when(i == k)(run)

        def first():
            for par in range(2):
                d = xdir(par)
                push(wx.at[p, xq, par], rxl.at[p, 0, par], xl_ss.at[p, 0, par], xl_rs.at[p, 0, par], {"x": mod(x + d, NX)})

        def second():
            push(wx.at[p, xq, 1], rxs.at[p, 1], xq_ss.at[p, 1], xq_rs.at[p, 1], {"x": xq})

        def third():
            push(wx.at[p, xq, 0], rxs.at[p, 0], xq_ss.at[p, 0], xq_rs.at[p, 0], {"x": xq})

        when(0, first)
        when(1, second)
        when(2, third)

    def start_z(p):
        for h in range(2):
            z_long(p, 0, h)
            z_short(p, 0, h)

    def take_g(p):
        o = offset(p)
        if p == 0:
            own_g.wait()
        for k in range(1, 3):
            arrived(gb.at[o, k], g_rs.at[o, k])
        for k in range(3):
            gt[k] = gb[o, k].astype(F32).T.astype(BF)

    def op_m(p, i):
        if i == 0:
            pass_on(0)
            take_g(0)
        if i < NX - 1:
            pass_on(i + 1)
        xq = order_x(i)
        arrived(xd.at[1 - c, xq], xo_rs.at[xq])
        for par in range(2):
            arrived(xd.at[3 - c, xq, par], xf_rs.at[xq, par])
        product(p, xq)
        after_product(p, i, xq)
        if i == 1:
            for o in (1, 3, 0):
                send_g(o)
        if i == 2:
            send_g(2)
        if i == NX - 1:
            start_z(p)

    def op_n(p):
        take_g(p)

        @pl.loop(0, NX)
        def _(i):
            xq = order_x(i)
            product(p, xq)
            after_product(p, i, xq)

        start_z(p)

    def z_long(p, k, h):
        d = xdir(h)
        push(
            wz.at[p, mod(z + (4 - k) * d, NZ), pl.ds(2 * h, 2)], rzl.at[p, k, h],
            zl_ss.at[p, k, h], zl_rs.at[p, k, h], {"z": mod(z + d, NZ)},
        )

    def z_short(p, k, h):
        d = xdir(h)
        push(
            wz.at[p, mod(z - (3 - k) * d, NZ), pl.ds(2 * h, 2)], rzs.at[p, k, h],
            zs_ss.at[p, k, h], zs_rs.at[p, k, h], {"z": mod(z - d, NZ)},
        )

    def z_long_add(p, k, h):
        t = mod(z + (3 - k) * xdir(h), NZ)
        arrived(rzl.at[p, k, h], zl_rs.at[p, k, h])
        for e in range(2):
            wz[p, t, 2 * h + e] = (wz[p, t, 2 * h + e].astype(F32) + rzl[p, k, h, e].astype(F32)).astype(BF)
        z_long(p, k + 1, h)

    def z_short_add(p, k, h):
        t = mod(z - (2 - k) * xdir(h), NZ)
        arrived(rzs.at[p, k, h], zs_rs.at[p, k, h])
        for e in range(2):
            wz[p, t, 2 * h + e] = (wz[p, t, 2 * h + e].astype(F32) + rzs[p, k, h, e].astype(F32)).astype(BF)
        z_short(p, k + 1, h)

    def pdir(p):
        return 1 - 2 * (p % 2)

    def z2_long(p, k, t):
        push(
            vb.at[p, t], r2zl.at[p, k], z2l_ss.at[p, k], z2l_rs.at[p, k], {"z": mod(z + pdir(p), NZ)}
        )

    def z2_short(p, k, t):
        push(
            vb.at[p, t], r2zs.at[p, k], z2s_ss.at[p, k], z2s_rs.at[p, k], {"z": mod(z - pdir(p), NZ)}
        )

    def z2_long_add(p, k):
        t = mod(z + (3 - k) * pdir(p), NZ)
        arrived(r2zl.at[p, k], z2l_rs.at[p, k])
        vb[p, t] = (vz[p, t] + r2zl[p, k].astype(F32)).astype(BF)
        z2_long(p, k + 1, t)

    def z2_short_add(p, k):
        t = mod(z - (2 - k) * pdir(p), NZ)
        arrived(r2zs.at[p, k], z2s_rs.at[p, k])
        vb[p, t] = (vz[p, t] + r2zs[p, k].astype(F32)).astype(BF)
        z2_short(p, k + 1, t)

    def op_xa(p, par):
        d = xdir(par)
        t = mod(x + d, NX)
        arrived(rxl.at[p, 0, par], xl_rs.at[p, 0, par])
        for j in range(4):
            wx[p, t, par, j] = (wx[p, t, par, j].astype(F32) + rxl[p, 0, par, j].astype(F32)).astype(BF)
        push(wx.at[p, t, par], rxl.at[p, 1, par], xl_ss.at[p, 1, par], xl_rs.at[p, 1, par], {"x": t})

    def op_xb(p):
        for par in range(2):
            arrived(rxs.at[p, par], xq_rs.at[p, par])
            arrived(rxl.at[p, 1, par], xl_rs.at[p, 1, par])
            for j in range(4):
                vz[p, 2 * j + par] = (
                    wx[p, x, par, j].astype(F32) + rxs[p, par, j].astype(F32) + rxl[p, 1, par, j].astype(F32)
                )
        d = pdir(p)
        t = mod(z + 4 * d, NZ)
        vb[p, t] = vz[p, t].astype(BF)
        z2_long(p, 0, t)
        t = mod(z - 3 * d, NZ)
        vb[p, t] = vz[p, t].astype(BF)
        z2_short(p, 0, t)

    def op_zb(p):
        for h in range(2):
            arrived(rzs.at[p, 2, h], zs_rs.at[p, 2, h])
            arrived(rzl.at[p, 3, h], zl_rs.at[p, 3, h])
            for e in range(2):
                uz[p, 2 * h + e] = (
                    wz[p, z, 2 * h + e].astype(F32) + rzs[p, 2, h, e].astype(F32) + rzl[p, 3, h, e].astype(F32)
                )
        d = pdir(p)
        t = mod(x + 2 * d, NX)
        ub[p, t] = uz[p, t].astype(BF)
        push(ub.at[p, t], r2xl.at[p, 0], x2l_ss.at[p, 0], x2l_rs.at[p, 0], {"x": mod(x + d, NX)})
        t = mod(x - d, NX)
        ub[p, t] = uz[p, t].astype(BF)
        push(ub.at[p, t], r2xs.at[p], x2s_ss.at[p], x2s_rs.at[p], {"x": t})

    def op_x2a(p):
        t = mod(x + pdir(p), NX)
        arrived(r2xl.at[p, 0], x2l_rs.at[p, 0])
        ub[p, t] = (uz[p, t] + r2xl[p, 0].astype(F32)).astype(BF)
        push(ub.at[p, t], r2xl.at[p, 1], x2l_ss.at[p, 1], x2l_rs.at[p, 1], {"x": t})

    s_mine = lax.rem(z + yl, 2)
    stays = s_mine == yl

    def op_f(p):
        arrived(r2xs.at[p], x2s_rs.at[p])
        arrived(r2xl.at[p, 1], x2l_rs.at[p, 1])
        arrived(r2zs.at[p, 2], z2s_rs.at[p, 2])
        arrived(r2zl.at[p, 3], z2l_rs.at[p, 3])
        ty[p, :RX] = vz[p, z] + r2zs[p, 2].astype(F32) + r2zl[p, 3].astype(F32)
        ty[p, RX:] = uz[p, x] + r2xs[p].astype(F32) + r2xl[p, 1].astype(F32)

        def remote():
            o = offset(p)
            push(ty.at[p], ry.at[o], y_ss.at[p], y_rs.at[o], {"yh": mod(yh + o, NH), "yl": s_mine})

        if p > 0:
            remote()
        else:
            pl.when(jnp.logical_not(stays))(remote)

            @pl.when(stays)
            def _():
                ry[0] = ty[0]

    ops = {
        "G": op_g, "M": op_m, "N": op_n, "xa": op_xa, "xb": op_xb, "zl": z_long_add, "zs": z_short_add,
        "z2l": z2_long_add, "z2s": z2_short_add, "zb": op_zb, "x2a": op_x2a, "f": op_f,
    }

    for name, *where in SEQUENCE:
        ops[name](*where)

    def settle(p):
        for k in (1, 2, 3) if p == 0 else (0, 1, 2) if p == 2 else (0, 1):
            sent(gb.at[p, 0], g_ss.at[p, k])
        for h in range(2):
            for k in range(2):
                sent(rxl.at[p, k, h], xl_ss.at[p, k, h])
            sent(rxs.at[p, h], xq_ss.at[p, h])
            for k in range(4):
                sent(rzl.at[p, k, h], zl_ss.at[p, k, h])
            for k in range(3):
                sent(rzs.at[p, k, h], zs_ss.at[p, k, h])
        for k in range(4):
            sent(r2zl.at[p, k], z2l_ss.at[p, k])
        for k in range(3):
            sent(r2zs.at[p, k], z2s_ss.at[p, k])
        for k in range(2):
            sent(r2xl.at[p, k], x2l_ss.at[p, k])
        sent(r2xs.at[p], x2s_ss.at[p])

    for q in range(NX):
        sent(xd.at[c, q], xo_ss.at[q])
        for par in range(2):
            sent(xs.at[q, par], xp_ss.at[q, par])
            sent(xs.at[q, par], xf_ss.at[q, par])
    settle(0)
    sent(gb.at[1, 0], g_ss.at[1 + 2 * yl, 2])

    for p in range(1, PHASES):
        arrived(ry.at[p], y_rs.at[p])

    @pl.when(jnp.logical_not(stays))
    def _():
        arrived(ry.at[0], y_rs.at[0])

    total = ry[0] + ry[1] + ry[2] + ry[3]
    part = jnp.sum(total * total, axis=0, keepdims=True)

    def spot(k, e):
        return mod(x + k, NX) * NC + mod(c + e, NC)

    nsrc[0] = part
    for k, e in x_line:
        push(nsrc.at[0], n1.at[spot(0, 0)], n1_ss.at[spot(k, e)], n1_rs.at[spot(0, 0)], x_dev(k, e))
    n1[spot(0, 0)] = part
    out_ref[...] = total.T
    settle(1)
    for k, e in x_line:
        arrived(n1.at[spot(k, e)], n1_rs.at[spot(k, e)])
    part = jnp.sum(n1[...], axis=0)

    nsrc[1] = part
    for k in range(1, NZ):
        t = mod(z + k, NZ)
        push(nsrc.at[1], n2.at[z], n2_ss.at[t], n2_rs.at[z], {"z": t})
    n2[z] = part
    settle(2)
    for k, e in x_line:
        sent(nsrc.at[0], n1_ss.at[spot(k, e)])
    for k in range(1, NZ):
        t = mod(z + k, NZ)
        arrived(n2.at[t], n2_rs.at[t])
    part = jnp.sum(n2[...], axis=0)

    def place(a, b):
        return mod(yh + a, NH) * NL + mod(yl + b, NL)

    nsrc[2] = part
    for a, b in y_line:
        push(nsrc.at[2], n3.at[place(0, 0)], n3_ss.at[place(a, b)], n3_rs.at[place(0, 0)], y_dev(a, b))
    n3[place(0, 0)] = part
    settle(3)
    for k in range(1, NZ):
        t = mod(z + k, NZ)
        sent(nsrc.at[1], n2_ss.at[t])

    @pl.when(jnp.logical_not(stays))
    def _():
        sent(ty.at[0], y_ss.at[0])

    for p in range(1, PHASES):
        sent(ty.at[p], y_ss.at[p])
    for a, b in y_line:
        arrived(n3.at[place(a, b)], n3_rs.at[place(a, b)])
    part = jnp.sum(n3[...], axis=0)
    whole = jnp.sum(part, axis=1, keepdims=True)
    out_ref[...] = out_ref[...] * jnp.minimum(jnp.float32(1.0), jnp.float32(limit) / jnp.sqrt(whole))
    for a, b in y_line:
        sent(nsrc.at[2], n3_ss.at[place(a, b)])


def body(stash_values, stash_scales, value_grad):
    tokens, width = stash_values.shape
    limit = math.sqrt(width * HD * lax.axis_size("yh") * lax.axis_size("c"))
    dma = pltpu.SemaphoreType.DMA
    pairs = [
        (NH, 4), (NX,), (NX, 2), (NX, 2),
        (PHASES, 2, 2), (PHASES, 2), (PHASES, 4, 2), (PHASES, 3, 2),
        (PHASES, 4), (PHASES, 3), (PHASES, 2), (PHASES,),
        (PHASES,), (NX * NC,), (NZ,), (NH * NL,),
    ]
    return pl.pallas_call(
        functools.partial(kernel, limit),
        out_shape=jax.ShapeDtypeStruct((HD, HD), F32),
        in_specs=[
            pl.BlockSpec(memory_space=pl.ANY),
            pl.BlockSpec(memory_space=pl.ANY),
            pl.BlockSpec(memory_space=pl.ANY),
        ],
        out_specs=pl.BlockSpec(memory_space=pltpu.VMEM),
        scratch_shapes=[
            pltpu.VMEM((tokens, width), BF),
            pltpu.VMEM((stash_scales.shape[1], tokens), BF),
            pltpu.VMEM((4, NX, 2, 4, TOK, HD), BF),
            pltpu.VMEM((NX, 2, 4, TOK, HD), BF),
            pltpu.VMEM((PHASES, 3, 2 * TOK, HD), BF),
            pltpu.VMEM((3, HD, 2 * TOK), BF),
            pltpu.VMEM((PHASES, NX, 2, 4, RX, HD), BF),
            pltpu.VMEM((PHASES, NZ, NX, RZ, HD), BF),
            pltpu.VMEM((PHASES, 2, 2, 4, RX, HD), BF),
            pltpu.VMEM((PHASES, 2, 4, RX, HD), BF),
            pltpu.VMEM((PHASES, 4, 2, 2, RZ, HD), BF),
            pltpu.VMEM((PHASES, 3, 2, 2, RZ, HD), BF),
            pltpu.VMEM((PHASES, NZ, RX, HD), F32),
            pltpu.VMEM((PHASES, NZ, RX, HD), BF),
            pltpu.VMEM((PHASES, NX, RZ, HD), F32),
            pltpu.VMEM((PHASES, NX, RZ, HD), BF),
            pltpu.VMEM((PHASES, 4, RX, HD), BF),
            pltpu.VMEM((PHASES, 3, RX, HD), BF),
            pltpu.VMEM((PHASES, 2, RZ, HD), BF),
            pltpu.VMEM((PHASES, RZ, HD), BF),
            pltpu.VMEM((PHASES, HD, HD), F32),
            pltpu.VMEM((PHASES, HD, HD), F32),
            pltpu.VMEM((3, 1, HD), F32),
            pltpu.VMEM((NX * NC, 1, HD), F32),
            pltpu.VMEM((NZ, 1, HD), F32),
            pltpu.VMEM((NH * NL, 1, HD), F32),
            dma((NX + 2,)),
            *(dma(shape) for pair in pairs for shape in (pair, pair)),
        ],
        compiler_params=pltpu.CompilerParams(
            collective_id=0, has_side_effects=True, vmem_limit_bytes=56 * 1024 * 1024
        ),
    )(stash_values, stash_scales.T, value_grad)


def solution(mesh):
    torus = Mesh(mesh.devices.reshape(NX, NZ, NL, NH, NC), AXES)
    rows = ("x", "z", "yl", "yh", "c")
    return jax.shard_map(
        body,
        mesh=torus,
        in_specs=(P(rows, None), P(rows, None), P(("x", "z", "yl"), ("yh", "c"))),
        out_specs=P(("x", "z", "yl"), ("yh", "c")),
        check_vma=False,
    )
```

time: 113 us -> 96.1 us (0.85)
  Pallas kernels: 110 us -> 93.6 us
  other arithmetic: 1.48 us -> 0 us
    pallas_call x1, Pallas kernels: 110 us -> 93.6 us  [body(): pl.pallas_call(functools.partial(kernel, limit), out_shape=jax.ShapeDtype...]
    mul x1 -> x0, other arithmetic: 1.48 us -> none  [body(): return total * jnp.minimum(jnp.float32(1.0), limit / jnp.sqrt(square[0, 0]))]
    unnamed x0 -> x1, local copies, waits for them, and re-layouts: none -> 1.47 us
    slice x1 -> x0, local copies, waits for them, and re-layouts: 1.19 us -> none  [body(): return total * jnp.minimum(jnp.float32(1.0), limit / jnp.sqrt(square[0, 0]))]
where the time goes in v2:
time: 96.1 us; the launch traced here: 95.1 us
  Pallas kernels  93.6 us (97%)
  local copies, waits for them, and re-layouts  1.47 us (2%)
    pallas_call x1, Pallas kernels, body(): pl.pallas_call(functools.partial(kernel, limit), out_shape=jax.ShapeDtype...  93.6 us

profile of v2, /device:TPU:1, one launch (start us, length us, event | category | flops | bytes accessed | tf_op | source)
XLA Modules:
  0.0 95.1 jit_solution(11494079851909693068)
XLA Ops:
  0.0 93.6 %shard_map.37 = f32[128,128]{1,0:T(8,128)} custom-call(bf16[128,8192]{1,0:T(8,128)(2,1)} %x_hbm.1, bf16[64,128]{1,0:T(8,128)(2,1)} %bitcast.1, bf16[1024,128]{1,0:T(8,128)(2,1)} %g_hbm.1), custom_call_target="tpu_custom_call" | custom-call | tf_op jit(solution)/shard_map/pallas_call | solution.py:511
  93.6 1.5 %copy.5 = f32[128,128]{1,0:T(8,128)} copy(f32[128,128]{1,0:T(8,128)} %shard_map.37) | data formatting | bytes 131072

commit v3 on v2

--- a/solution.py
+++ b/solution.py
@@ -43,12 +43,11 @@
 def kernel(
     limit, x_hbm, s_hbm, g_hbm, out_ref,
     xv, sv, xd, xs, gb, gt, wx, wz,
-    rxl, rxs, rzl, rzs, vz, vb, uz, ub,
-    r2zl, r2zs, r2xl, r2xs, ty, ry, nsrc, n1, n2, n3,
-    ld_sem, g_ss, g_rs, xo_ss, xo_rs, xp_ss, xp_rs, xf_ss, xf_rs,
-    xl_ss, xl_rs, xq_ss, xq_rs, zl_ss, zl_rs, zs_ss, zs_rs,
-    z2l_ss, z2l_rs, z2s_ss, z2s_rs, x2l_ss, x2l_rs, x2s_ss, x2s_rs,
-    y_ss, y_rs, n1_ss, n1_rs, n2_ss, n2_rs, n3_ss, n3_rs,
+    rxl, rxb, rzl, rzs, rzf, vz, vb, uz, ub,
+    r2zl, r2zs, r2x, f2z, f2x, ty, ry, nsrc, n1, n2, n3,
+    ld_sem, out_sem, rs_sem, g_own, g_rs, xo_rs, xp_rs, xf_rs,
+    xl_rs, xb_rs, zl_rs, zs_rs, zf_rs, z2l_rs, z2s_rs, x2_rs, fz_rs, fx_rs,
+    y_rs, n_rs,
 ):
     x, z, yl, yh, c = (lax.axis_index(name) for name in AXES)
     quarter = NZ * 2 * HD
@@ -120,24 +119,24 @@
         return jnp.where(yl == 1, p, NH - p)
 
     def send_first_g():
-        push(slab(yh), gb.at[0, 1], g_ss.at[0, 1], g_rs.at[0, 1], beside)
-        push(slab(yh + 1 - 2 * yl), gb.at[0, 2], g_ss.at[0, 3], g_rs.at[0, 2], beside)
+        push(slab(yh), gb.at[0, 1], out_sem.at[1], g_rs.at[0], beside)
+        push(slab(yh + 1 - 2 * yl), gb.at[0, 2], out_sem.at[1], g_rs.at[0], beside)
 
     def send_g(o):
         if o == 0:
-            push(slab(yh), gb.at[1 + 2 * yl, 2], g_ss.at[0, 2], g_rs.at[1 + 2 * yl, 2], beyond)
+            push(slab(yh), gb.at[1 + 2 * yl, 2], out_sem.at[1], g_rs.at[1 + 2 * yl], beyond)
         else:
             user = mod(yh - o, NH)
-            push(slab(user), gb.at[o, 0], g_ss.at[o, 0], g_rs.at[o, 0], {"yh": user})
+            push(slab(user), gb.at[o, 0], out_sem.at[1], g_own.at[o], {"yh": user})
 
     def op_g(o):
-        arrived(gb.at[o, 0], g_rs.at[o, 0])
-        push(gb.at[o, 0], gb.at[o, 1], g_ss.at[o, 1], g_rs.at[o, 1], beside)
+        arrived(gb.at[o, 0], g_own.at[o])
+        push(gb.at[o, 0], gb.at[o, 1], out_sem.at[1], g_rs.at[o], beside)
         other = mod(o + 1 - 2 * yl, NH)
 
         @pl.when(other > 0)
         def _():
-            push(gb.at[o, 0], gb.at[other, 2], g_ss.at[o, 2], g_rs.at[other, 2], beyond)
+            push(gb.at[o, 0], gb.at[other, 2], out_sem.at[1], g_rs.at[other], beyond)
 
     scale_load.wait()
     scales = sv[...].astype(F32).T.astype(BF)
@@ -158,7 +157,7 @@
             par, j = lax.rem(zq, 2), zq // 2
             s = lax.rem(zq + yl, 2)
             b = (xq * NZ + zq) * 2
-            xs[xq, par, j] = dequant(b + 1 - s)
+            xs[xq * 8 + par * 4 + j] = dequant(b + 1 - s)
             xd[c, xq, par, j] = dequant(b + s)
 
     def share(i):
@@ -166,13 +165,17 @@
         for par in range(2):
             s_out = lax.rem(par + yl + 1, 2)
             partner = {"yh": mod(yh + s_out * (2 * yl - 1), NH), "yl": 1 - yl}
-            push(xs.at[xq, par], xd.at[2 + c, xq, par], xp_ss.at[xq, par], xp_rs.at[xq, par], partner)
-        push(xd.at[c, xq], xd.at[c, xq], xo_ss.at[xq], xo_rs.at[xq], {"c": 1 - c})
+            push(xs.at[pl.ds(xq * 8 + par * 4, 4)], xd.at[2 + c, xq, par], out_sem.at[0], xp_rs.at[xq, par], partner)
+
+    def share_chip(i):
+        xq = order_x(i)
+        push(xd.at[c, xq], xd.at[c, xq], out_sem.at[0], xo_rs.at[xq], {"c": 1 - c})
 
     prepare(0)
     pl.semaphore_wait(barrier, len(x_line) + NZ - 1 + len(y_line))
     share(0)
     send_first_g()
+    share_chip(0)
 
     @pl.loop(1, NX)
     def _(i):
@@ -186,7 +189,7 @@
         for k in range(2):
             par = lax.rem(near + k, 2)
             arrived(xd.at[2 + c, xq, par], xp_rs.at[xq, par])
-            push(xd.at[2 + c, xq, par], xd.at[2 + c, xq, par], xf_ss.at[xq, par], xf_rs.at[xq, par], {"c": 1 - c})
+            push(xd.at[2 + c, xq, par], xd.at[2 + c, xq, par], out_sem.at[0], xf_rs.at[xq], {"c": 1 - c})
 
     def product(p, xq):
         for par in range(2):
@@ -220,13 +223,13 @@
         def first():
             for par in range(2):
                 d = xdir(par)
-                push(wx.at[p, xq, par], rxl.at[p, 0, par], xl_ss.at[p, 0, par], xl_rs.at[p, 0, par], {"x": mod(x + d, NX)})
+                push(wx.at[p, xq, par], rxl.at[p, par], rs_sem.at[p], xl_rs.at[p, par], {"x": mod(x + d, NX)})
 
         def second():
-            push(wx.at[p, xq, 1], rxs.at[p, 1], xq_ss.at[p, 1], xq_rs.at[p, 1], {"x": xq})
+            push(wx.at[p, xq, 1], rxb.at[p, 3], rs_sem.at[p], xb_rs.at[p], {"x": xq})
 
         def third():
-            push(wx.at[p, xq, 0], rxs.at[p, 0], xq_ss.at[p, 0], xq_rs.at[p, 0], {"x": xq})
+            push(wx.at[p, xq, 0], rxb.at[p, 2], rs_sem.at[p], xb_rs.at[p], {"x": xq})
 
         when(0, first)
         when(1, second)
@@ -241,23 +244,24 @@
         o = offset(p)
         if p == 0:
             own_g.wait()
-        for k in range(1, 3):
-            arrived(gb.at[o, k], g_rs.at[o, k])
+        arrived(gb.at[o, pl.ds(1, 2)], g_rs.at[o])
         for k in range(3):
             gt[k] = gb[o, k].astype(F32).T.astype(BF)
 
     def op_m(p, i):
         if i == 0:
             pass_on(0)
+            share_chip(1)
             take_g(0)
+        xq = order_x(i)
+        arrived(xd.at[1 - c, xq], xo_rs.at[xq])
+        arrived(xd.at[3 - c, xq], xf_rs.at[xq])
+        product(p, xq)
+        after_product(p, i, xq)
         if i < NX - 1:
             pass_on(i + 1)
-        xq = order_x(i)
-        arrived(xd.at[1 - c, xq], xo_rs.at[xq])
-        for par in range(2):
-            arrived(xd.at[3 - c, xq, par], xf_rs.at[xq, par])
-        product(p, xq)
-        after_product(p, i, xq)
+            if i < NX - 2:
+                share_chip(i + 2)
         if i == 1:
             for o in (1, 3, 0):
                 send_g(o)
@@ -279,17 +283,15 @@
 
     def z_long(p, k, h):
         d = xdir(h)
-        push(
-            wz.at[p, mod(z + (4 - k) * d, NZ), pl.ds(2 * h, 2)], rzl.at[p, k, h],
-            zl_ss.at[p, k, h], zl_rs.at[p, k, h], {"z": mod(z + d, NZ)},
-        )
+        dst, rs = (rzf.at[p, h], zf_rs.at[p]) if k == 3 else (rzl.at[p, k, h], zl_rs.at[p, k, h])
+        src = wz.at[p, mod(z + (4 - k) * d, NZ), pl.ds(2 * h, 2)]
+        push(src, dst, rs_sem.at[p], rs, {"z": mod(z + d, NZ)})
 
     def z_short(p, k, h):
         d = xdir(h)
-        push(
-            wz.at[p, mod(z - (3 - k) * d, NZ), pl.ds(2 * h, 2)], rzs.at[p, k, h],
-            zs_ss.at[p, k, h], zs_rs.at[p, k, h], {"z": mod(z - d, NZ)},
-        )
+        dst, rs = (rzf.at[p, 2 + h], zf_rs.at[p]) if k == 2 else (rzs.at[p, k, h], zs_rs.at[p, k, h])
+        src = wz.at[p, mod(z - (3 - k) * d, NZ), pl.ds(2 * h, 2)]
+        push(src, dst, rs_sem.at[p], rs, {"z": mod(z - d, NZ)})
 
     def z_long_add(p, k, h):
         t = mod(z + (3 - k) * xdir(h), NZ)
@@ -309,14 +311,12 @@
         return 1 - 2 * (p % 2)
 
     def z2_long(p, k, t):
-        push(
-            vb.at[p, t], r2zl.at[p, k], z2l_ss.at[p, k], z2l_rs.at[p, k], {"z": mod(z + pdir(p), NZ)}
-        )
+        dst, rs = (f2z.at[p, 0], fz_rs.at[p]) if k == 3 else (r2zl.at[p, k], z2l_rs.at[p, k])
+        push(vb.at[p, t], dst, rs_sem.at[p], rs, {"z": mod(z + pdir(p), NZ)})
 
     def z2_short(p, k, t):
-        push(
-            vb.at[p, t], r2zs.at[p, k], z2s_ss.at[p, k], z2s_rs.at[p, k], {"z": mod(z - pdir(p), NZ)}
-        )
+        dst, rs = (f2z.at[p, 1], fz_rs.at[p]) if k == 2 else (r2zs.at[p, k], z2s_rs.at[p, k])
+        push(vb.at[p, t], dst, rs_sem.at[p], rs, {"z": mod(z - pdir(p), NZ)})
 
     def z2_long_add(p, k):
         t = mod(z + (3 - k) * pdir(p), NZ)
@@ -333,18 +333,17 @@
     def op_xa(p, par):
         d = xdir(par)
         t = mod(x + d, NX)
-        arrived(rxl.at[p, 0, par], xl_rs.at[p, 0, par])
+        arrived(rxl.at[p, par], xl_rs.at[p, par])
         for j in range(4):
-            wx[p, t, par, j] = (wx[p, t, par, j].astype(F32) + rxl[p, 0, par, j].astype(F32)).astype(BF)
-        push(wx.at[p, t, par], rxl.at[p, 1, par], xl_ss.at[p, 1, par], xl_rs.at[p, 1, par], {"x": t})
+            wx[p, t, par, j] = (wx[p, t, par, j].astype(F32) + rxl[p, par, j].astype(F32)).astype(BF)
+        push(wx.at[p, t, par], rxb.at[p, par], rs_sem.at[p], xb_rs.at[p], {"x": t})
 
     def op_xb(p):
+        arrived(rxb.at[p], xb_rs.at[p])
         for par in range(2):
-            arrived(rxs.at[p, par], xq_rs.at[p, par])
-            arrived(rxl.at[p, 1, par], xl_rs.at[p, 1, par])
             for j in range(4):
                 vz[p, 2 * j + par] = (
-                    wx[p, x, par, j].astype(F32) + rxs[p, par, j].astype(F32) + rxl[p, 1, par, j].astype(F32)
+                    wx[p, x, par, j].astype(F32) + rxb[p, 2 + par, j].astype(F32) + rxb[p, par, j].astype(F32)
                 )
         d = pdir(p)
         t = mod(z + 4 * d, NZ)
@@ -355,41 +354,39 @@
         z2_short(p, 0, t)
 
     def op_zb(p):
+        arrived(rzf.at[p], zf_rs.at[p])
         for h in range(2):
-            arrived(rzs.at[p, 2, h], zs_rs.at[p, 2, h])
-            arrived(rzl.at[p, 3, h], zl_rs.at[p, 3, h])
             for e in range(2):
                 uz[p, 2 * h + e] = (
-                    wz[p, z, 2 * h + e].astype(F32) + rzs[p, 2, h, e].astype(F32) + rzl[p, 3, h, e].astype(F32)
+                    wz[p, z, 2 * h + e].astype(F32) + rzf[p, 2 + h, e].astype(F32) + rzf[p, h, e].astype(F32)
                 )
         d = pdir(p)
         t = mod(x + 2 * d, NX)
         ub[p, t] = uz[p, t].astype(BF)
-        push(ub.at[p, t], r2xl.at[p, 0], x2l_ss.at[p, 0], x2l_rs.at[p, 0], {"x": mod(x + d, NX)})
+        push(ub.at[p, t], r2x.at[p], rs_sem.at[p], x2_rs.at[p], {"x": mod(x + d, NX)})
         t = mod(x - d, NX)
         ub[p, t] = uz[p, t].astype(BF)
-        push(ub.at[p, t], r2xs.at[p], x2s_ss.at[p], x2s_rs.at[p], {"x": t})
+        push(ub.at[p, t], f2x.at[p, 1], rs_sem.at[p], fx_rs.at[p], {"x": t})
 
     def op_x2a(p):
         t = mod(x + pdir(p), NX)
-        arrived(r2xl.at[p, 0], x2l_rs.at[p, 0])
-        ub[p, t] = (uz[p, t] + r2xl[p, 0].astype(F32)).astype(BF)
-        push(ub.at[p, t], r2xl.at[p, 1], x2l_ss.at[p, 1], x2l_rs.at[p, 1], {"x": t})
+        arrived(r2x.at[p], x2_rs.at[p])
+        ub[p, t] = (uz[p, t] + r2x[p].astype(F32)).astype(BF)
+        push(ub.at[p, t], f2x.at[p, 0], rs_sem.at[p], fx_rs.at[p], {"x": t})
 
     s_mine = lax.rem(z + yl, 2)
     stays = s_mine == yl
 
     def op_f(p):
-        arrived(r2xs.at[p], x2s_rs.at[p])
-        arrived(r2xl.at[p, 1], x2l_rs.at[p, 1])
-        arrived(r2zs.at[p, 2], z2s_rs.at[p, 2])
-        arrived(r2zl.at[p, 3], z2l_rs.at[p, 3])
-        ty[p, :RX] = vz[p, z] + r2zs[p, 2].astype(F32) + r2zl[p, 3].astype(F32)
-        ty[p, RX:] = uz[p, x] + r2xs[p].astype(F32) + r2xl[p, 1].astype(F32)
+        arrived(f2x.at[p], fx_rs.at[p])
+        arrived(f2z.at[p], fz_rs.at[p])
+        ty[p, :RX] = vz[p, z] + f2z[p, 0].astype(F32) + f2z[p, 1].astype(F32)
+        ty[p, RX:] = uz[p, x] + f2x[p, 0].astype(F32) + f2x[p, 1].astype(F32)
+        far = 1 if p > 0 else 0
 
         def remote():
             o = offset(p)
-            push(ty.at[p], ry.at[o], y_ss.at[p], y_rs.at[o], {"yh": mod(yh + o, NH), "yl": s_mine})
+            push(ty.at[p], ry.at[o], out_sem.at[2 + far], y_rs.at[far], {"yh": mod(yh + o, NH), "yl": s_mine})
 
         if p > 0:
             remote()
@@ -408,35 +405,11 @@
     for name, *where in SEQUENCE:
         ops[name](*where)
 
-    def settle(p):
-        for k in (1, 2, 3) if p == 0 else (0, 1, 2) if p == 2 else (0, 1):
-            sent(gb.at[p, 0], g_ss.at[p, k])
-        for h in range(2):
-            for k in range(2):
-                sent(rxl.at[p, k, h], xl_ss.at[p, k, h])
-            sent(rxs.at[p, h], xq_ss.at[p, h])
-            for k in range(4):
-                sent(rzl.at[p, k, h], zl_ss.at[p, k, h])
-            for k in range(3):
-                sent(rzs.at[p, k, h], zs_ss.at[p, k, h])
-        for k in range(4):
-            sent(r2zl.at[p, k], z2l_ss.at[p, k])
-        for k in range(3):
-            sent(r2zs.at[p, k], z2s_ss.at[p, k])
-        for k in range(2):
-            sent(r2xl.at[p, k], x2l_ss.at[p, k])
-        sent(r2xs.at[p], x2s_ss.at[p])
-
-    for q in range(NX):
-        sent(xd.at[c, q], xo_ss.at[q])
-        for par in range(2):
-            sent(xs.at[q, par], xp_ss.at[q, par])
-            sent(xs.at[q, par], xf_ss.at[q, par])
-    settle(0)
-    sent(gb.at[1, 0], g_ss.at[1 + 2 * yl, 2])
-
-    for p in range(1, PHASES):
-        arrived(ry.at[p], y_rs.at[p])
+    sent(xd.at[pl.ds(0, 3)], out_sem.at[0])
+    sent(xs.at[pl.ds(0, 22)], out_sem.at[1])
+    for p in range(PHASES):
+        sent(xs.at[pl.ds(0, 31)], rs_sem.at[p])
+    arrived(ry.at[pl.ds(1, PHASES - 1)], y_rs.at[1])
 
     @pl.when(jnp.logical_not(stays))
     def _():
@@ -450,25 +423,19 @@
 
     nsrc[0] = part
     for k, e in x_line:
-        push(nsrc.at[0], n1.at[spot(0, 0)], n1_ss.at[spot(k, e)], n1_rs.at[spot(0, 0)], x_dev(k, e))
+        push(nsrc.at[0], n1.at[spot(0, 0)], out_sem.at[4], n_rs.at[0], x_dev(k, e))
     n1[spot(0, 0)] = part
     out_ref[...] = total.T
-    settle(1)
-    for k, e in x_line:
-        arrived(n1.at[spot(k, e)], n1_rs.at[spot(k, e)])
+    arrived(n1.at[pl.ds(0, len(x_line))], n_rs.at[0])
     part = jnp.sum(n1[...], axis=0)
 
     nsrc[1] = part
     for k in range(1, NZ):
         t = mod(z + k, NZ)
-        push(nsrc.at[1], n2.at[z], n2_ss.at[t], n2_rs.at[z], {"z": t})
+        push(nsrc.at[1], n2.at[z], out_sem.at[5], n_rs.at[1], {"z": t})
     n2[z] = part
-    settle(2)
-    for k, e in x_line:
-        sent(nsrc.at[0], n1_ss.at[spot(k, e)])
-    for k in range(1, NZ):
-        t = mod(z + k, NZ)
-        arrived(n2.at[t], n2_rs.at[t])
+    sent(n1.at[pl.ds(0, len(x_line))], out_sem.at[4])
+    arrived(n2.at[pl.ds(0, NZ - 1)], n_rs.at[1])
     part = jnp.sum(n2[...], axis=0)
 
     def place(a, b):
@@ -476,38 +443,26 @@
 
     nsrc[2] = part
     for a, b in y_line:
-        push(nsrc.at[2], n3.at[place(0, 0)], n3_ss.at[place(a, b)], n3_rs.at[place(0, 0)], y_dev(a, b))
+        push(nsrc.at[2], n3.at[place(0, 0)], out_sem.at[6], n_rs.at[2], y_dev(a, b))
     n3[place(0, 0)] = part
-    settle(3)
-    for k in range(1, NZ):
-        t = mod(z + k, NZ)
-        sent(nsrc.at[1], n2_ss.at[t])
+    sent(n2.at[pl.ds(0, NZ - 1)], out_sem.at[5])
 
     @pl.when(jnp.logical_not(stays))
     def _():
-        sent(ty.at[0], y_ss.at[0])
-
-    for p in range(1, PHASES):
-        sent(ty.at[p], y_ss.at[p])
-    for a, b in y_line:
-        arrived(n3.at[place(a, b)], n3_rs.at[place(a, b)])
+        sent(ty.at[0], out_sem.at[2])
+
+    sent(ty.at[pl.ds(1, PHASES - 1)], out_sem.at[3])
+    arrived(n3.at[pl.ds(0, len(y_line))], n_rs.at[2])
     part = jnp.sum(n3[...], axis=0)
     whole = jnp.sum(part, axis=1, keepdims=True)
     out_ref[...] = out_ref[...] * jnp.minimum(jnp.float32(1.0), jnp.float32(limit) / jnp.sqrt(whole))
-    for a, b in y_line:
-        sent(nsrc.at[2], n3_ss.at[place(a, b)])
+    sent(n3.at[pl.ds(0, len(y_line))], out_sem.at[6])
 
 
 def body(stash_values, stash_scales, value_grad):
     tokens, width = stash_values.shape
     limit = math.sqrt(width * HD * lax.axis_size("yh") * lax.axis_size("c"))
     dma = pltpu.SemaphoreType.DMA
-    pairs = [
-        (NH, 4), (NX,), (NX, 2), (NX, 2),
-        (PHASES, 2, 2), (PHASES, 2), (PHASES, 4, 2), (PHASES, 3, 2),
-        (PHASES, 4), (PHASES, 3), (PHASES, 2), (PHASES,),
-        (PHASES,), (NX * NC,), (NZ,), (NH * NL,),
-    ]
     return pl.pallas_call(
         functools.partial(kernel, limit),
         out_shape=jax.ShapeDtypeStruct((HD, HD), F32),
@@ -521,23 +476,25 @@
             pltpu.VMEM((tokens, width), BF),
             pltpu.VMEM((stash_scales.shape[1], tokens), BF),
             pltpu.VMEM((4, NX, 2, 4, TOK, HD), BF),
-            pltpu.VMEM((NX, 2, 4, TOK, HD), BF),
-            pltpu.VMEM((PHASES, 3, 2 * TOK, HD), BF),
+            pltpu.VMEM((NX * 8, TOK, HD), BF),
+            pltpu.VMEM((NH, 3, 2 * TOK, HD), BF),
             pltpu.VMEM((3, HD, 2 * TOK), BF),
             pltpu.VMEM((PHASES, NX, 2, 4, RX, HD), BF),
             pltpu.VMEM((PHASES, NZ, NX, RZ, HD), BF),
-            pltpu.VMEM((PHASES, 2, 2, 4, RX, HD), BF),
             pltpu.VMEM((PHASES, 2, 4, RX, HD), BF),
-            pltpu.VMEM((PHASES, 4, 2, 2, RZ, HD), BF),
+            pltpu.VMEM((PHASES, 4, 4, RX, HD), BF),
             pltpu.VMEM((PHASES, 3, 2, 2, RZ, HD), BF),
+            pltpu.VMEM((PHASES, 2, 2, 2, RZ, HD), BF),
+            pltpu.VMEM((PHASES, 4, 2, RZ, HD), BF),
             pltpu.VMEM((PHASES, NZ, RX, HD), F32),
             pltpu.VMEM((PHASES, NZ, RX, HD), BF),
             pltpu.VMEM((PHASES, NX, RZ, HD), F32),
             pltpu.VMEM((PHASES, NX, RZ, HD), BF),
-            pltpu.VMEM((PHASES, 4, RX, HD), BF),
             pltpu.VMEM((PHASES, 3, RX, HD), BF),
+            pltpu.VMEM((PHASES, 2, RX, HD), BF),
+            pltpu.VMEM((PHASES, RZ, HD), BF),
+            pltpu.VMEM((PHASES, 2, RX, HD), BF),
             pltpu.VMEM((PHASES, 2, RZ, HD), BF),
-            pltpu.VMEM((PHASES, RZ, HD), BF),
             pltpu.VMEM((PHASES, HD, HD), F32),
             pltpu.VMEM((PHASES, HD, HD), F32),
             pltpu.VMEM((3, 1, HD), F32),
@@ -545,7 +502,25 @@
             pltpu.VMEM((NZ, 1, HD), F32),
             pltpu.VMEM((NH * NL, 1, HD), F32),
             dma((NX + 2,)),
-            *(dma(shape) for pair in pairs for shape in (pair, pair)),
+            dma((7,)),
+            dma((PHASES,)),
+            dma((NH,)),
+            dma((NH,)),
+            dma((NX,)),
+            dma((NX, 2)),
+            dma((NX,)),
+            dma((PHASES, 2)),
+            dma((PHASES,)),
+            dma((PHASES, 3, 2)),
+            dma((PHASES, 2, 2)),
+            dma((PHASES,)),
+            dma((PHASES, 3)),
+            dma((PHASES, 2)),
+            dma((PHASES,)),
+            dma((PHASES,)),
+            dma((PHASES,)),
+            dma((2,)),
+            dma((3,)),
         ],
         compiler_params=pltpu.CompilerParams(
             collective_id=0, has_side_effects=True, vmem_limit_bytes=56 * 1024 * 1024

time: 96.1 us -> 93.4 us (0.972)
  Pallas kernels: 93.6 us -> 91 us
    pallas_call x1, Pallas kernels: 93.6 us -> 91 us  [body(): pl.pallas_call(functools.partial(kernel, limit), out_shape=jax.ShapeDtype...]
where the time goes in v3:
time: 93.4 us; the launch traced here: 92.4 us
  Pallas kernels  91 us (97%)
  local copies, waits for them, and re-layouts  1.47 us (2%)
    pallas_call x1, Pallas kernels, body(): pl.pallas_call(functools.partial(kernel, limit), out_shape=jax.ShapeDtype...  91 us

profile of v3, /device:TPU:1, one launch (start us, length us, event | category | flops | bytes accessed | tf_op | source)
XLA Modules:
  0.0 92.4 jit_solution(3088732429589041079)
XLA Ops:
  0.0 91.0 %shard_map.37 = f32[128,128]{1,0:T(8,128)} custom-call(bf16[128,8192]{1,0:T(8,128)(2,1)} %x_hbm.1, bf16[64,128]{1,0:T(8,128)(2,1)} %bitcast.1, bf16[1024,128]{1,0:T(8,128)(2,1)} %g_hbm.1), custom_call_target="tpu_custom_call" | custom-call | tf_op jit(solution)/shard_map/pallas_call | solution.py:466
  91.0 1.5 %copy.5 = f32[128,128]{1,0:T(8,128)} copy(f32[128,128]{1,0:T(8,128)} %shard_map.37) | data formatting | bytes 131072

commit v4 on v3

--- a/solution.py
+++ b/solution.py
@@ -14,23 +14,24 @@
 AXES = ("x", "z", "yl", "yh", "c")
 HD = 128
 TOK = 128
-RX = 80
-RZ = HD - RX
+ROWS = (80, 80, 80, 80)
 PHASES = NH
+TREE = (2, 3)
 SEQUENCE = (
-    ("M", 0, 0), ("M", 0, 1), ("xa", 0, 0), ("M", 0, 2), ("xa", 0, 1), ("M", 0, 3), ("G", 1), ("G", 3), ("zl", 0, 0, 0),
-    ("zs", 0, 0, 0), ("xb", 0), ("zl", 0, 0, 1), ("zs", 0, 0, 1), ("N", 1), ("G", 2), ("z2l", 0, 0), ("z2s", 0, 0),
-    ("zl", 0, 1, 0), ("zs", 0, 1, 0), ("zs", 0, 1, 1), ("zl", 0, 1, 1), ("N", 2), ("z2l", 0, 1), ("z2s", 0, 1),
-    ("zl", 0, 2, 0), ("xa", 1, 0), ("xa", 1, 1), ("zl", 1, 0, 0), ("zl", 0, 2, 1), ("zs", 1, 0, 0), ("zl", 1, 0, 1),
-    ("zs", 1, 0, 1), ("N", 3), ("z2l", 0, 2), ("zb", 0), ("xa", 2, 0), ("xa", 2, 1), ("zl", 2, 0, 0),
-    ("zl", 1, 1, 0), ("zs", 1, 1, 0), ("zs", 2, 0, 0), ("zl", 2, 0, 1), ("zs", 2, 0, 1), ("zl", 1, 1, 1),
-    ("zs", 1, 1, 1), ("zl", 3, 0, 0), ("zs", 3, 0, 0), ("zl", 3, 0, 1), ("zs", 3, 0, 1), ("xb", 1), ("zl", 2, 1, 0),
-    ("zs", 2, 1, 0), ("zl", 1, 2, 0), ("zl", 2, 1, 1), ("zs", 2, 1, 1), ("zl", 1, 2, 1), ("xa", 3, 0), ("xa", 3, 1),
-    ("zs", 3, 1, 0), ("zl", 3, 1, 0), ("zl", 3, 1, 1), ("z2l", 1, 0), ("zs", 3, 1, 1), ("z2s", 1, 0), ("x2a", 0),
-    ("zl", 2, 2, 0), ("zl", 2, 2, 1), ("zb", 1), ("xb", 2), ("zl", 3, 2, 0), ("zl", 3, 2, 1), ("z2l", 1, 1),
-    ("z2s", 1, 1), ("zb", 2), ("xb", 3), ("f", 0), ("x2a", 1), ("z2l", 2, 0), ("z2s", 2, 0), ("zb", 3),
-    ("z2l", 1, 2), ("x2a", 2), ("z2l", 3, 0), ("z2s", 3, 0), ("z2l", 2, 1), ("z2s", 2, 1), ("x2a", 3), ("f", 1),
-    ("z2l", 3, 1), ("z2s", 3, 1), ("z2l", 2, 2), ("z2l", 3, 2), ("f", 2), ("f", 3),
+    ("M", 0, 0), ("M", 0, 1), ("xa", 0, 0), ("M", 0, 2), ("G", 0), ("xa", 0, 1), ("M", 0, 3), ("G", 1), ("G", 2),
+    ("zl", 0, 0, 0), ("zs", 0, 0, 0), ("N", 1), ("G", 3), ("G", 4), ("xb", 0), ("zl", 0, 1, 0), ("zs", 0, 1, 0),
+    ("zl", 0, 0, 1), ("zs", 0, 0, 1), ("N", 2), ("z2l", 0, 0), ("z2s", 0, 0), ("zl", 0, 2, 0), ("xa", 1, 0),
+    ("xa", 1, 1), ("zl", 0, 1, 1), ("zs", 0, 1, 1), ("zl", 1, 0, 0), ("zs", 1, 0, 0), ("zl", 1, 0, 1),
+    ("zs", 1, 0, 1), ("N", 3), ("zl", 2, 0, 0), ("z2l", 0, 1), ("z2s", 0, 1), ("xa", 2, 0), ("xa", 2, 1),
+    ("zs", 2, 0, 0), ("zl", 0, 2, 1), ("zl", 2, 0, 1), ("zs", 2, 0, 1), ("zs", 1, 1, 0), ("zl", 1, 1, 0),
+    ("zl", 1, 1, 1), ("zs", 1, 1, 1), ("zs", 3, 0, 0), ("zl", 3, 0, 0), ("zl", 3, 0, 1), ("zs", 3, 0, 1),
+    ("zs", 2, 1, 0), ("zl", 2, 1, 0), ("xb", 1), ("z2l", 0, 2), ("zb", 0), ("zs", 2, 1, 1), ("zl", 2, 1, 1),
+    ("zl", 1, 2, 0), ("xa", 3, 0), ("xa", 3, 1), ("zl", 1, 2, 1), ("zl", 3, 1, 0), ("zs", 3, 1, 0), ("zs", 3, 1, 1),
+    ("zl", 3, 1, 1), ("zl", 2, 2, 0), ("z2s", 1, 0), ("z2l", 1, 0), ("fz", 0), ("zl", 2, 2, 1), ("xb", 2),
+    ("x2a", 0), ("zb", 1), ("zl", 3, 2, 0), ("zl", 3, 2, 1), ("z2l", 1, 1), ("zb", 2), ("xb", 3), ("fx", 0),
+    ("x2a", 1), ("z2s", 1, 1), ("zt", 2, 0), ("zt", 2, 2), ("zt", 2, 1), ("zb", 3), ("z2l", 1, 2), ("x2a", 2),
+    ("zt", 3, 0), ("zt", 3, 2), ("fx", 1), ("zt", 3, 1), ("x2a", 3), ("fx", 2), ("fz", 1), ("fz", 2), ("fx", 3),
+    ("fz", 3),
 )
 BF = jnp.bfloat16
 F32 = jnp.float32
@@ -41,16 +42,19 @@
 
 
 def kernel(
-    limit, x_hbm, s_hbm, g_hbm, out_ref,
-    xv, sv, xd, xs, gb, gt, wx, wz,
-    rxl, rxb, rzl, rzs, rzf, vz, vb, uz, ub,
-    r2zl, r2zs, r2x, f2z, f2x, ty, ry, nsrc, n1, n2, n3,
-    ld_sem, out_sem, rs_sem, g_own, g_rs, xo_rs, xp_rs, xf_rs,
-    xl_rs, xb_rs, zl_rs, zs_rs, zf_rs, z2l_rs, z2s_rs, x2_rs, fz_rs, fx_rs,
-    y_rs, n_rs,
+    limit, x_hbm, s_hbm, g_hbm, out_ref, *scratch
 ):
     x, z, yl, yh, c = (lax.axis_index(name) for name in AXES)
     quarter = NZ * 2 * HD
+    xv, sv, xd, xs, gb, gt, ty, ry, nsrc, n1, n2, n3 = scratch[:12]
+    (
+        ld_sem, out_sem, rs_sem, g_own, g_rs, xo_rs, xp_rs, xf_rs,
+        xl_rs, xb_rs, zl_rs, zs_rs, zf_rs, z2l_rs, z2s_rs, x2_rs, fz_rs, fx_rs,
+        y_rs, n_rs,
+    ) = scratch[12:32]
+    (
+        wx, wz, rxl, rxb, rzl, rzs, rzf, vz, vb, uz, ub, r2zl, r2zs, r2x, f2z, f2x,
+    ) = (scratch[32 + k :: 16] for k in range(16))
 
     def push(src, dst, ss, rs, dev):
         pltpu.make_async_remote_copy(
@@ -129,14 +133,23 @@
             user = mod(yh - o, NH)
             push(slab(user), gb.at[o, 0], out_sem.at[1], g_own.at[o], {"yh": user})
 
-    def op_g(o):
-        arrived(gb.at[o, 0], g_own.at[o])
-        push(gb.at[o, 0], gb.at[o, 1], out_sem.at[1], g_rs.at[o], beside)
-        other = mod(o + 1 - 2 * yl, NH)
-
-        @pl.when(other > 0)
-        def _():
-            push(gb.at[o, 0], gb.at[other, 2], out_sem.at[1], g_rs.at[other], beyond)
+    soon = 1 + 2 * yl
+    late = 3 - 2 * yl
+
+    def op_g(k):
+        if k == 0:
+            arrived(gb.at[soon, 0], g_own.at[soon])
+            push(gb.at[soon, 0], gb.at[soon, 1], out_sem.at[1], g_rs.at[soon], beside)
+        elif k == 1:
+            arrived(gb.at[late, 0], g_own.at[late])
+        elif k == 2:
+            push(gb.at[soon, 0], gb.at[2, 2], out_sem.at[1], g_rs.at[2], beyond)
+        elif k == 3:
+            arrived(gb.at[2, 0], g_own.at[2])
+            push(gb.at[2, 0], gb.at[2, 1], out_sem.at[1], g_rs.at[2], beside)
+        else:
+            push(gb.at[late, 0], gb.at[late, 1], out_sem.at[1], g_rs.at[late], beside)
+            push(gb.at[2, 0], gb.at[3 - 2 * yl, 2], out_sem.at[1], g_rs.at[3 - 2 * yl], beyond)
 
     scale_load.wait()
     scales = sv[...].astype(F32).T.astype(BF)
@@ -191,7 +204,7 @@
             arrived(xd.at[2 + c, xq, par], xp_rs.at[xq, par])
             push(xd.at[2 + c, xq, par], xd.at[2 + c, xq, par], out_sem.at[0], xf_rs.at[xq], {"c": 1 - c})
 
-    def product(p, xq):
+    def product(p, i, xq):
         for par in range(2):
             s = lax.rem(par + yl, 2)
             lhs = jnp.concatenate([gt[0], gt[1 + s]], axis=1)
@@ -206,8 +219,8 @@
                 res = jnp.dot(lhs, rhs, preferred_element_type=F32).astype(BF)
                 for e in range(2):
                     j = 2 * jj + e
-                    wx[p, xq, par, j] = res[:RX, e * HD : (e + 1) * HD]
-                    wz[p, 2 * j + par, xq] = res[RX:, e * HD : (e + 1) * HD]
+                    wx[p][xq, par, j] = res[: ROWS[p], e * HD : (e + 1) * HD]
+                    wz[p][2 * j + par, i] = res[ROWS[p] :, e * HD : (e + 1) * HD]
 
     def xdir(par):
         return 1 - 2 * par
@@ -223,22 +236,23 @@
         def first():
             for par in range(2):
                 d = xdir(par)
-                push(wx.at[p, xq, par], rxl.at[p, par], rs_sem.at[p], xl_rs.at[p, par], {"x": mod(x + d, NX)})
+                push(wx[p].at[xq, par], rxl[p].at[par], rs_sem.at[p], xl_rs.at[p, par], {"x": mod(x + d, NX)})
 
         def second():
-            push(wx.at[p, xq, 1], rxb.at[p, 3], rs_sem.at[p], xb_rs.at[p], {"x": xq})
+            push(wx[p].at[xq, 1], rxb[p].at[3], rs_sem.at[p], xb_rs.at[p], {"x": xq})
 
         def third():
-            push(wx.at[p, xq, 0], rxb.at[p, 2], rs_sem.at[p], xb_rs.at[p], {"x": xq})
+            push(wx[p].at[xq, 0], rxb[p].at[2], rs_sem.at[p], xb_rs.at[p], {"x": xq})
 
         when(0, first)
         when(1, second)
+        when(1, lambda: start_z(p, 0))
         when(2, third)
-
-    def start_z(p):
-        for h in range(2):
-            z_long(p, 0, h)
-            z_short(p, 0, h)
+        when(3, lambda: start_z(p, 1))
+
+    def start_z(p, h):
+        z_long(p, 0, h)
+        z_short(p, 0, h)
 
     def take_g(p):
         o = offset(p)
@@ -256,19 +270,17 @@
         xq = order_x(i)
         arrived(xd.at[1 - c, xq], xo_rs.at[xq])
         arrived(xd.at[3 - c, xq], xf_rs.at[xq])
-        product(p, xq)
+        product(p, i, xq)
         after_product(p, i, xq)
         if i < NX - 1:
             pass_on(i + 1)
             if i < NX - 2:
                 share_chip(i + 2)
-        if i == 1:
+        if i == 0:
             for o in (1, 3, 0):
                 send_g(o)
-        if i == 2:
+        if i == 1:
             send_g(2)
-        if i == NX - 1:
-            start_z(p)
 
     def op_n(p):
         take_g(p)
@@ -276,117 +288,140 @@
         @pl.loop(0, NX)
         def _(i):
             xq = order_x(i)
-            product(p, xq)
+            product(p, i, xq)
             after_product(p, i, xq)
-
-        start_z(p)
 
     def z_long(p, k, h):
         d = xdir(h)
-        dst, rs = (rzf.at[p, h], zf_rs.at[p]) if k == 3 else (rzl.at[p, k, h], zl_rs.at[p, k, h])
-        src = wz.at[p, mod(z + (4 - k) * d, NZ), pl.ds(2 * h, 2)]
+        dst, rs = (rzf[p].at[h], zf_rs.at[p]) if k == 3 else (rzl[p].at[k, h], zl_rs.at[p, k, h])
+        src = wz[p].at[mod(z + (4 - k) * d, NZ), pl.ds(2 * h, 2)]
         push(src, dst, rs_sem.at[p], rs, {"z": mod(z + d, NZ)})
 
     def z_short(p, k, h):
         d = xdir(h)
-        dst, rs = (rzf.at[p, 2 + h], zf_rs.at[p]) if k == 2 else (rzs.at[p, k, h], zs_rs.at[p, k, h])
-        src = wz.at[p, mod(z - (3 - k) * d, NZ), pl.ds(2 * h, 2)]
+        dst, rs = (rzf[p].at[2 + h], zf_rs.at[p]) if k == 2 else (rzs[p].at[k, h], zs_rs.at[p, k, h])
+        src = wz[p].at[mod(z - (3 - k) * d, NZ), pl.ds(2 * h, 2)]
         push(src, dst, rs_sem.at[p], rs, {"z": mod(z - d, NZ)})
 
     def z_long_add(p, k, h):
         t = mod(z + (3 - k) * xdir(h), NZ)
-        arrived(rzl.at[p, k, h], zl_rs.at[p, k, h])
+        arrived(rzl[p].at[k, h], zl_rs.at[p, k, h])
         for e in range(2):
-            wz[p, t, 2 * h + e] = (wz[p, t, 2 * h + e].astype(F32) + rzl[p, k, h, e].astype(F32)).astype(BF)
+            wz[p][t, 2 * h + e] = (wz[p][t, 2 * h + e].astype(F32) + rzl[p][k, h, e].astype(F32)).astype(BF)
         z_long(p, k + 1, h)
 
     def z_short_add(p, k, h):
         t = mod(z - (2 - k) * xdir(h), NZ)
-        arrived(rzs.at[p, k, h], zs_rs.at[p, k, h])
+        arrived(rzs[p].at[k, h], zs_rs.at[p, k, h])
         for e in range(2):
-            wz[p, t, 2 * h + e] = (wz[p, t, 2 * h + e].astype(F32) + rzs[p, k, h, e].astype(F32)).astype(BF)
+            wz[p][t, 2 * h + e] = (wz[p][t, 2 * h + e].astype(F32) + rzs[p][k, h, e].astype(F32)).astype(BF)
         z_short(p, k + 1, h)
 
     def pdir(p):
         return 1 - 2 * (p % 2)
 
     def z2_long(p, k, t):
-        dst, rs = (f2z.at[p, 0], fz_rs.at[p]) if k == 3 else (r2zl.at[p, k], z2l_rs.at[p, k])
-        push(vb.at[p, t], dst, rs_sem.at[p], rs, {"z": mod(z + pdir(p), NZ)})
+        dst, rs = (f2z[p].at[0], fz_rs.at[p]) if k == 3 else (r2zl[p].at[k], z2l_rs.at[p, k])
+        push(vb[p].at[t], dst, rs_sem.at[p], rs, {"z": mod(z + pdir(p), NZ)})
 
     def z2_short(p, k, t):
-        dst, rs = (f2z.at[p, 1], fz_rs.at[p]) if k == 2 else (r2zs.at[p, k], z2s_rs.at[p, k])
-        push(vb.at[p, t], dst, rs_sem.at[p], rs, {"z": mod(z - pdir(p), NZ)})
+        dst, rs = (f2z[p].at[1], fz_rs.at[p]) if k == 2 else (r2zs[p].at[k], z2s_rs.at[p, k])
+        push(vb[p].at[t], dst, rs_sem.at[p], rs, {"z": mod(z - pdir(p), NZ)})
 
     def z2_long_add(p, k):
         t = mod(z + (3 - k) * pdir(p), NZ)
-        arrived(r2zl.at[p, k], z2l_rs.at[p, k])
-        vb[p, t] = (vz[p, t] + r2zl[p, k].astype(F32)).astype(BF)
+        arrived(r2zl[p].at[k], z2l_rs.at[p, k])
+        vb[p][t] = (vz[p][t] + r2zl[p][k].astype(F32)).astype(BF)
         z2_long(p, k + 1, t)
 
     def z2_short_add(p, k):
         t = mod(z - (2 - k) * pdir(p), NZ)
-        arrived(r2zs.at[p, k], z2s_rs.at[p, k])
-        vb[p, t] = (vz[p, t] + r2zs[p, k].astype(F32)).astype(BF)
+        arrived(r2zs[p].at[k], z2s_rs.at[p, k])
+        vb[p][t] = (vz[p][t] + r2zs[p][k].astype(F32)).astype(BF)
         z2_short(p, k + 1, t)
 
     def op_xa(p, par):
         d = xdir(par)
         t = mod(x + d, NX)
-        arrived(rxl.at[p, par], xl_rs.at[p, par])
+        arrived(rxl[p].at[par], xl_rs.at[p, par])
         for j in range(4):
-            wx[p, t, par, j] = (wx[p, t, par, j].astype(F32) + rxl[p, par, j].astype(F32)).astype(BF)
-        push(wx.at[p, t, par], rxb.at[p, par], rs_sem.at[p], xb_rs.at[p], {"x": t})
+            wx[p][t, par, j] = (wx[p][t, par, j].astype(F32) + rxl[p][par, j].astype(F32)).astype(BF)
+        push(wx[p].at[t, par], rxb[p].at[par], rs_sem.at[p], xb_rs.at[p], {"x": t})
 
     def op_xb(p):
-        arrived(rxb.at[p], xb_rs.at[p])
+        arrived(rxb[p], xb_rs.at[p])
         for par in range(2):
             for j in range(4):
-                vz[p, 2 * j + par] = (
-                    wx[p, x, par, j].astype(F32) + rxb[p, 2 + par, j].astype(F32) + rxb[p, par, j].astype(F32)
+                vz[p][2 * j + par] = (
+                    wx[p][x, par, j].astype(F32) + rxb[p][2 + par, j].astype(F32) + rxb[p][par, j].astype(F32)
+                )
+        if p in TREE:
+            start_tree(p)
+            return
+        d = pdir(p)
+        t = mod(z + 4 * d, NZ)
+        vb[p][t] = vz[p][t].astype(BF)
+        z2_long(p, 0, t)
+        t = mod(z - 3 * d, NZ)
+        vb[p][t] = vz[p][t].astype(BF)
+        z2_short(p, 0, t)
+
+    def op_zb(p):
+        arrived(rzf[p], zf_rs.at[p])
+        for h in range(2):
+            for e in range(2):
+                uz[p][2 * h + e] = (
+                    wz[p][z, 2 * h + e].astype(F32) + rzf[p][2 + h, e].astype(F32) + rzf[p][h, e].astype(F32)
                 )
         d = pdir(p)
-        t = mod(z + 4 * d, NZ)
-        vb[p, t] = vz[p, t].astype(BF)
-        z2_long(p, 0, t)
-        t = mod(z - 3 * d, NZ)
-        vb[p, t] = vz[p, t].astype(BF)
-        z2_short(p, 0, t)
-
-    def op_zb(p):
-        arrived(rzf.at[p], zf_rs.at[p])
-        for h in range(2):
-            for e in range(2):
-                uz[p, 2 * h + e] = (
-                    wz[p, z, 2 * h + e].astype(F32) + rzf[p, 2 + h, e].astype(F32) + rzf[p, h, e].astype(F32)
-                )
-        d = pdir(p)
-        t = mod(x + 2 * d, NX)
-        ub[p, t] = uz[p, t].astype(BF)
-        push(ub.at[p, t], r2x.at[p], rs_sem.at[p], x2_rs.at[p], {"x": mod(x + d, NX)})
-        t = mod(x - d, NX)
-        ub[p, t] = uz[p, t].astype(BF)
-        push(ub.at[p, t], f2x.at[p, 1], rs_sem.at[p], fx_rs.at[p], {"x": t})
+        ub[p][0] = uz[p][0].astype(BF)
+        push(ub[p].at[0], r2x[p], rs_sem.at[p], x2_rs.at[p], {"x": mod(x + d, NX)})
+        k = 2 - p % 2
+        ub[p][k] = uz[p][k].astype(BF)
+        push(ub[p].at[k], f2x[p].at[1], rs_sem.at[p], fx_rs.at[p], {"x": mod(x - d, NX)})
 
     def op_x2a(p):
-        t = mod(x + pdir(p), NX)
-        arrived(r2x.at[p], x2_rs.at[p])
-        ub[p, t] = (uz[p, t] + r2x[p].astype(F32)).astype(BF)
-        push(ub.at[p, t], f2x.at[p, 0], rs_sem.at[p], fx_rs.at[p], {"x": t})
+        k = 1 + p % 2
+        arrived(r2x[p], x2_rs.at[p])
+        ub[p][k] = (uz[p][k] + r2x[p][...].astype(F32)).astype(BF)
+        push(ub[p].at[k], f2x[p].at[0], rs_sem.at[p], fx_rs.at[p], {"x": mod(x + pdir(p), NX)})
 
     s_mine = lax.rem(z + yl, 2)
     stays = s_mine == yl
 
-    def op_f(p):
-        arrived(f2x.at[p], fx_rs.at[p])
-        arrived(f2z.at[p], fz_rs.at[p])
-        ty[p, :RX] = vz[p, z] + f2z[p, 0].astype(F32) + f2z[p, 1].astype(F32)
-        ty[p, RX:] = uz[p, x] + f2x[p, 0].astype(F32) + f2x[p, 1].astype(F32)
+    def z_tree(p, k):
+        d = pdir(p)
+        if k == 0:
+            t, got, rs, slot = mod(z + 3 * d, NZ), r2zl[p].at[0], z2l_rs.at[p, 0], 0
+        elif k == 1:
+            t, got, rs, slot = mod(z + d, NZ), r2zl[p].at[1], z2l_rs.at[p, 1], 1
+        else:
+            t, got, rs, slot = mod(z - 2 * d, NZ), r2zs[p].at[0], z2s_rs.at[p, 0], 2
+        arrived(got, rs)
+        vb[p][t] = (vz[p][t] + got[...].astype(F32)).astype(BF)
+        push(vb[p].at[t], f2z[p].at[slot], rs_sem.at[p], fz_rs.at[p], {"z": t})
+
+    def start_tree(p):
+        d = pdir(p)
+        near, back = {"z": mod(z + d, NZ)}, {"z": mod(z - d, NZ)}
+        for steps, dst, rs, dev in (
+            (4, r2zl[p].at[0], z2l_rs.at[p, 0], near),
+            (-3, r2zs[p].at[0], z2s_rs.at[p, 0], back),
+            (2, r2zl[p].at[1], z2l_rs.at[p, 1], near),
+            (-1, f2z[p].at[3], fz_rs.at[p], back),
+        ):
+            t = mod(z + steps * d, NZ)
+            vb[p][t] = vz[p][t].astype(BF)
+            push(vb[p].at[t], dst, rs_sem.at[p], rs, dev)
+
+    def give(p, first, rows):
+        part = pl.ds(first, rows)
         far = 1 if p > 0 else 0
 
         def remote():
             o = offset(p)
-            push(ty.at[p], ry.at[o], out_sem.at[2 + far], y_rs.at[far], {"yh": mod(yh + o, NH), "yl": s_mine})
+            dev = {"yh": mod(yh + o, NH), "yl": s_mine}
+            push(ty.at[p, part], ry.at[o, part], out_sem.at[2 + far], y_rs.at[far], dev)
 
         if p > 0:
             remote()
@@ -395,11 +430,24 @@
 
             @pl.when(stays)
             def _():
-                ry[0] = ty[0]
+                ry[0, part] = ty[0, part]
+
+    def op_fx(p):
+        arrived(f2x[p], fx_rs.at[p])
+        ty[p, ROWS[p] :] = uz[p][3] + f2x[p][0].astype(F32) + f2x[p][1].astype(F32)
+        give(p, ROWS[p], HD - ROWS[p])
+
+    def op_fz(p):
+        arrived(f2z[p], fz_rs.at[p])
+        total = vz[p][z]
+        for k in range(f2z[p].shape[0]):
+            total += f2z[p][k].astype(F32)
+        ty[p, : ROWS[p]] = total
+        give(p, 0, ROWS[p])
 
     ops = {
         "G": op_g, "M": op_m, "N": op_n, "xa": op_xa, "xb": op_xb, "zl": z_long_add, "zs": z_short_add,
-        "z2l": z2_long_add, "z2s": z2_short_add, "zb": op_zb, "x2a": op_x2a, "f": op_f,
+        "z2l": z2_long_add, "z2s": z2_short_add, "zb": op_zb, "x2a": op_x2a, "fx": op_fx, "fz": op_fz, "zt": z_tree,
     }
 
     for name, *where in SEQUENCE:
@@ -457,6 +505,14 @@
     whole = jnp.sum(part, axis=1, keepdims=True)
     out_ref[...] = out_ref[...] * jnp.minimum(jnp.float32(1.0), jnp.float32(limit) / jnp.sqrt(whole))
     sent(n3.at[pl.ds(0, len(y_line))], out_sem.at[6])
+
+
+def phase_scratch(rx, rz, last):
+    shapes = [
+        (NX, 2, 4, rx), (NZ, NX, rz), (2, 4, rx), (4, 4, rx), (3, 2, 2, rz), (2, 2, 2, rz), (4, 2, rz),
+        (NZ, rx), (NZ, rx), (NX, rz), (NX, rz), (3, rx), (2, rx), (rz,), (last, rx), (2, rz),
+    ]
+    return [pltpu.VMEM((*s, HD), F32 if k in (7, 9) else BF) for k, s in enumerate(shapes)]
 
 
 def body(stash_values, stash_scales, value_grad):
@@ -479,22 +535,6 @@
             pltpu.VMEM((NX * 8, TOK, HD), BF),
             pltpu.VMEM((NH, 3, 2 * TOK, HD), BF),
             pltpu.VMEM((3, HD, 2 * TOK), BF),
-            pltpu.VMEM((PHASES, NX, 2, 4, RX, HD), BF),
-            pltpu.VMEM((PHASES, NZ, NX, RZ, HD), BF),
-            pltpu.VMEM((PHASES, 2, 4, RX, HD), BF),
-            pltpu.VMEM((PHASES, 4, 4, RX, HD), BF),
-            pltpu.VMEM((PHASES, 3, 2, 2, RZ, HD), BF),
-            pltpu.VMEM((PHASES, 2, 2, 2, RZ, HD), BF),
-            pltpu.VMEM((PHASES, 4, 2, RZ, HD), BF),
-            pltpu.VMEM((PHASES, NZ, RX, HD), F32),
-            pltpu.VMEM((PHASES, NZ, RX, HD), BF),
-            pltpu.VMEM((PHASES, NX, RZ, HD), F32),
-            pltpu.VMEM((PHASES, NX, RZ, HD), BF),
-            pltpu.VMEM((PHASES, 3, RX, HD), BF),
-            pltpu.VMEM((PHASES, 2, RX, HD), BF),
-            pltpu.VMEM((PHASES, RZ, HD), BF),
-            pltpu.VMEM((PHASES, 2, RX, HD), BF),
-            pltpu.VMEM((PHASES, 2, RZ, HD), BF),
             pltpu.VMEM((PHASES, HD, HD), F32),
             pltpu.VMEM((PHASES, HD, HD), F32),
             pltpu.VMEM((3, 1, HD), F32),
@@ -521,6 +561,7 @@
             dma((PHASES,)),
             dma((2,)),
             dma((3,)),
+            *(ref for p, rows in enumerate(ROWS) for ref in phase_scratch(rows, HD - rows, 4 if p in TREE else 2)),
         ],
         compiler_params=pltpu.CompilerParams(
             collective_id=0, has_side_effects=True, vmem_limit_bytes=56 * 1024 * 1024

time: 93.4 us -> 86.2 us (0.923)
  Pallas kernels: 91 us -> 83.8 us
    pallas_call x1, Pallas kernels: 91 us -> 83.8 us  [body(): pl.pallas_call(functools.partial(kernel, limit), out_shape=jax.ShapeDtype...]
where the time goes in v4:
time: 86.2 us; the launch traced here: 85.3 us
  Pallas kernels  83.8 us (97%)
  local copies, waits for them, and re-layouts  1.47 us (2%)
    pallas_call x1, Pallas kernels, body(): pl.pallas_call(functools.partial(kernel, limit), out_shape=jax.ShapeDtype...  83.8 us

profile of v4, /device:TPU:1, one launch (start us, length us, event | category | flops | bytes accessed | tf_op | source)
XLA Modules:
  0.0 85.3 jit_solution(9774749840641213338)
XLA Ops:
  0.0 83.8 %shard_map.37 = f32[128,128]{1,0:T(8,128)} custom-call(bf16[128,8192]{1,0:T(8,128)(2,1)} %x_hbm.1, bf16[64,128]{1,0:T(8,128)(2,1)} %bitcast.1, bf16[1024,128]{1,0:T(8,128)(2,1)} %g_hbm.1), custom_call_target="tpu_custom_call" | custom-call | tf_op jit(solution)/shard_map/pallas_call | solution.py:522
  83.8 1.5 %copy.5 = f32[128,128]{1,0:T(8,128)} copy(f32[128,128]{1,0:T(8,128)} %shard_map.37) | data formatting | bytes 131072

commit v5 on v4

--- a/solution.py
+++ b/solution.py
@@ -19,7 +19,7 @@
 TREE = (2, 3)
 SEQUENCE = (
     ("M", 0, 0), ("M", 0, 1), ("xa", 0, 0), ("M", 0, 2), ("G", 0), ("xa", 0, 1), ("M", 0, 3), ("G", 1), ("G", 2),
-    ("zl", 0, 0, 0), ("zs", 0, 0, 0), ("N", 1), ("G", 3), ("G", 4), ("xb", 0), ("zl", 0, 1, 0), ("zs", 0, 1, 0),
+    ("zl", 0, 0, 0), ("zs", 0, 0, 0), ("G", 3), ("N", 1), ("G", 4), ("xb", 0), ("zl", 0, 1, 0), ("zs", 0, 1, 0),
     ("zl", 0, 0, 1), ("zs", 0, 0, 1), ("N", 2), ("z2l", 0, 0), ("z2s", 0, 0), ("zl", 0, 2, 0), ("xa", 1, 0),
     ("xa", 1, 1), ("zl", 0, 1, 1), ("zs", 0, 1, 1), ("zl", 1, 0, 0), ("zs", 1, 0, 0), ("zl", 1, 0, 1),
     ("zs", 1, 0, 1), ("N", 3), ("zl", 2, 0, 0), ("z2l", 0, 1), ("z2s", 0, 1), ("xa", 2, 0), ("xa", 2, 1),
@@ -91,19 +91,18 @@
     def greet(dev):
         pl.semaphore_signal(barrier, inc=1, device_id=dev, device_id_type=MESH)
 
-    x_line = [(k, e) for k in range(NX) for e in range(NC) if (k, e) != (0, 0)]
+    plane = [(k, e, w) for k in range(NX) for e in range(NC) for w in range(NZ) if (k, e, w) != (0, 0, 0)]
     y_line = [(a, b) for a in range(NH) for b in range(NL) if (a, b) != (0, 0)]
 
-    def x_dev(k, e):
-        return {"x": mod(x + k, NX), "c": mod(c + e, NC)}
+    def plane_dev(k, e, w):
+        return {"x": mod(x + k, NX), "c": mod(c + e, NC), "z": mod(z + w, NZ)}
 
     def y_dev(a, b):
         return {"yh": mod(yh + a, NH), "yl": mod(yl + b, NL)}
 
-    for k, e in x_line:
-        greet(x_dev(k, e))
-    for k in range(1, NZ):
-        greet({"z": mod(z + k, NZ)})
+    met = [step for step in plane if step[2] == 0 or step[:2] == (0, 0)]
+    for step in met:
+        greet(plane_dev(*step))
     for a, b in y_line:
         greet(y_dev(a, b))
 
@@ -185,7 +184,7 @@
         push(xd.at[c, xq], xd.at[c, xq], out_sem.at[0], xo_rs.at[xq], {"c": 1 - c})
 
     prepare(0)
-    pl.semaphore_wait(barrier, len(x_line) + NZ - 1 + len(y_line))
+    pl.semaphore_wait(barrier, len(met) + len(y_line))
     share(0)
     send_first_g()
     share_chip(0)
@@ -466,25 +465,17 @@
     total = ry[0] + ry[1] + ry[2] + ry[3]
     part = jnp.sum(total * total, axis=0, keepdims=True)
 
-    def spot(k, e):
-        return mod(x + k, NX) * NC + mod(c + e, NC)
-
+    def spot(k, e, w):
+        return (mod(x + k, NX) * NC + mod(c + e, NC)) * NZ + mod(z + w, NZ)
+
+    mine = spot(0, 0, 0)
     nsrc[0] = part
-    for k, e in x_line:
-        push(nsrc.at[0], n1.at[spot(0, 0)], out_sem.at[4], n_rs.at[0], x_dev(k, e))
-    n1[spot(0, 0)] = part
+    for step in plane:
+        push(nsrc.at[0], n1.at[mine], out_sem.at[4], n_rs.at[0], plane_dev(*step))
+    n1[mine] = part
     out_ref[...] = total.T
-    arrived(n1.at[pl.ds(0, len(x_line))], n_rs.at[0])
+    arrived(n1.at[pl.ds(0, len(plane))], n_rs.at[0])
     part = jnp.sum(n1[...], axis=0)
-
-    nsrc[1] = part
-    for k in range(1, NZ):
-        t = mod(z + k, NZ)
-        push(nsrc.at[1], n2.at[z], out_sem.at[5], n_rs.at[1], {"z": t})
-    n2[z] = part
-    sent(n1.at[pl.ds(0, len(x_line))], out_sem.at[4])
-    arrived(n2.at[pl.ds(0, NZ - 1)], n_rs.at[1])
-    part = jnp.sum(n2[...], axis=0)
 
     def place(a, b):
         return mod(yh + a, NH) * NL + mod(yl + b, NL)
@@ -493,7 +484,7 @@
     for a, b in y_line:
         push(nsrc.at[2], n3.at[place(0, 0)], out_sem.at[6], n_rs.at[2], y_dev(a, b))
     n3[place(0, 0)] = part
-    sent(n2.at[pl.ds(0, NZ - 1)], out_sem.at[5])
+    sent(n1.at[pl.ds(0, len(plane))], out_sem.at[4])
 
     @pl.when(jnp.logical_not(stays))
     def _():
@@ -538,7 +529,7 @@
             pltpu.VMEM((PHASES, HD, HD), F32),
             pltpu.VMEM((PHASES, HD, HD), F32),
             pltpu.VMEM((3, 1, HD), F32),
-            pltpu.VMEM((NX * NC, 1, HD), F32),
+            pltpu.VMEM((NX * NC * NZ, 1, HD), F32),
             pltpu.VMEM((NZ, 1, HD), F32),
             pltpu.VMEM((NH * NL, 1, HD), F32),
             dma((NX + 2,)),

time: 86.2 us -> 84.3 us (0.978)
  Pallas kernels: 83.8 us -> 82.6 us
    pallas_call x1, Pallas kernels: 83.8 us -> 82.6 us  [body(): pl.pallas_call(functools.partial(kernel, limit), out_shape=jax.ShapeDtype...]
where the time goes in v5:
time: 84.3 us; the launch traced here: 84.1 us
  Pallas kernels  82.6 us (98%)
  local copies, waits for them, and re-layouts  1.47 us (2%)
    pallas_call x1, Pallas kernels, body(): pl.pallas_call(functools.partial(kernel, limit), out_shape=jax.ShapeDtype...  82.6 us

profile of v5, /device:TPU:1, one launch (start us, length us, event | category | flops | bytes accessed | tf_op | source)
XLA Modules:
  0.0 84.1 jit_solution(6804258819773359814)
XLA Ops:
  0.0 82.6 %shard_map.37 = f32[128,128]{1,0:T(8,128)} custom-call(bf16[128,8192]{1,0:T(8,128)(2,1)} %x_hbm.1, bf16[64,128]{1,0:T(8,128)(2,1)} %bitcast.1, bf16[1024,128]{1,0:T(8,128)(2,1)} %g_hbm.1), custom_call_target="tpu_custom_call" | custom-call | tf_op jit(solution)/shard_map/pallas_call | solution.py:513
  82.6 1.5 %copy.5 = f32[128,128]{1,0:T(8,128)} copy(f32[128,128]{1,0:T(8,128)} %shard_map.37) | data formatting | bytes 131072

commit v6 on v5

--- a/solution.py
+++ b/solution.py
@@ -100,7 +100,7 @@
     def y_dev(a, b):
         return {"yh": mod(yh + a, NH), "yl": mod(yl + b, NL)}
 
-    met = [step for step in plane if step[2] == 0 or step[:2] == (0, 0)]
+    met = [(1, 0, 0), (NX - 1, 0, 0), (0, 1, 0), (0, 0, 1), (0, 0, NZ - 1)]
     for step in met:
         greet(plane_dev(*step))
     for a, b in y_line:

time: 84.3 us -> 83.5 us (level)
  no operation moved by 1% of the time
where the time goes in v6:
time: 83.5 us; the launch traced here: 83.4 us
  Pallas kernels  81.9 us (98%)
  local copies, waits for them, and re-layouts  1.47 us (2%)
    pallas_call x1, Pallas kernels, body(): pl.pallas_call(functools.partial(kernel, limit), out_shape=jax.ShapeDtype...  81.9 us

profile of v6, /device:TPU:1, one launch (start us, length us, event | category | flops | bytes accessed | tf_op | source)
XLA Modules:
  0.0 83.4 jit_solution(8937358085343380883)
XLA Ops:
  0.0 81.9 %shard_map.37 = f32[128,128]{1,0:T(8,128)} custom-call(bf16[128,8192]{1,0:T(8,128)(2,1)} %x_hbm.1, bf16[64,128]{1,0:T(8,128)(2,1)} %bitcast.1, bf16[1024,128]{1,0:T(8,128)(2,1)} %g_hbm.1), custom_call_target="tpu_custom_call" | custom-call | tf_op jit(solution)/shard_map/pallas_call | solution.py:513
  81.9 1.5 %copy.5 = f32[128,128]{1,0:T(8,128)} copy(f32[128,128]{1,0:T(8,128)} %shard_map.37) | data formatting | bytes 131072
